TPU v7x, 512 devices: a whole 4x4x16 slice. The times are simulated.
512 devices in a mesh: ctx: 64 (over x, z), tp: 8 (over y, core).
Axes of the slice: x: 4, y: 4, z: 16, core: 2. Of those that a mesh axis runs over, the one named last changes fastest.
Arguments:
- queries: bfloat16 [16384, 128, 128], P('ctx', 'tp'), may hold values from -80 to 80
- keys: bfloat16 [16384, 8, 128], P(('ctx', 'tp')), may hold values from -4 to 4
- values: bfloat16 [16384, 8, 128], P(('ctx', 'tp')), may hold values from -6 to 6
- output_gradient: bfloat16 [16384, 128, 128], P('ctx', 'tp'), may hold values from -6 to 6
- doc_blocks: int32 [64], replicated, may hold values from 1 to 5, 128 in all
Outputs:
- query_grads: bfloat16 [16384, 128, 128], P('ctx', 'tp')
- key_gradient: bfloat16 [16384, 8, 128], P(('ctx', 'tp'))
- value_gradient: bfloat16 [16384, 8, 128], P(('ctx', 'tp'))
Inputs may be any that keep to these rules, and one draw needn't show every extreme that they name: `doc_blocks`: document lengths in blocks of 128 tokens; they sum to 128 and the longest has exactly 5 blocks.
All inputs are finite; a program needn't handle non-finite values.
Results may differ from a plain program's by a relative error of at most 0.0082.
Values may be sent and summed in bfloat16 or wider, within the bound.
No kernel may reach another device: no remote copies, remote signals or barrier semaphores. Data moves between devices by JAX's collectives and lax.ppermute only.
A program may use at most 128 MiB of HBM per device.

v0:
```python
from functools import reduce
import math

import jax
import jax.numpy as jnp
from jax import lax
from jax.sharding import PartitionSpec as P

BLK = 128
SPAN = 2
BLK_DEV = 2


def passed_along(block, axis, distance):
    devices = range(lax.axis_size(axis))
    route = [(i - distance, i) for i in devices if i - distance in devices]
    return lax.ppermute(block, axis, route)


def on_device(queries, keys, values, output_gradient, doc_blocks):
    tok_count = queries.shape[0]
    heads_local = queries.shape[1]
    head_size = queries.shape[2]
    scale = 1.0 / math.sqrt(head_size)
    key_local, value_local = (
        lax.all_to_all(keys, "tp", split_axis=1, concat_axis=0, tiled=True),
        lax.all_to_all(values, "tp", split_axis=1, concat_axis=0, tiled=True),
    )
    groups = key_local.shape[1]
    group_ratio = heads_local // groups
    query_group = queries.reshape(tok_count, groups, group_ratio, head_size)
    grad_group = output_gradient.reshape(tok_count, groups, group_ratio, head_size)
    place = lax.axis_index("ctx")
    ends = jnp.cumsum(doc_blocks)

    def block_doc(blocks):
        return jnp.sum((ends[None, :] <= blocks[:, None]).astype(jnp.int32), axis=1)

    local_tok = place * tok_count + jnp.arange(tok_count, dtype=jnp.int32)
    query_doc = block_doc(local_tok // BLK)
    first_doc = block_doc(jnp.reshape(place * BLK_DEV, (1,)))[0]
    sources = [(key_local, value_local)]
    for distance in range(1, SPAN + 1):
        sources.append(passed_along((key_local, value_local), "ctx", distance))
    masks = []
    links = []
    for distance in range(SPAN + 1):
        key_tok = local_tok - distance * tok_count
        key_doc = block_doc(key_tok // BLK)
        allowed = (
            (query_doc[:, None] == key_doc[None, :])
            & (key_tok[None, :] <= local_tok[:, None])
            & (key_tok[None, :] >= 0)
        )
        masks.append(allowed)
        if distance == 0:
            links.append(jnp.asarray(True))
        else:
            last_block = jnp.reshape((place - distance) * BLK_DEV + BLK_DEV - 1, (1,))
            links.append((place - distance >= 0) & (block_doc(last_block)[0] == first_doc))
    scores = []
    for distance in range(SPAN + 1):
        key_part = sources[distance][0]

        def compute_scores(key_part=key_part, allowed=masks[distance]):
            raw = (
                jnp.einsum(
                    "qgrd,kgd->grqk", query_group, key_part, preferred_element_type=jnp.float32
                )
                * scale
            )
            return jnp.where(allowed[None, None], raw, -1e30)

        scores.append(compute_scores())
    top = reduce(jnp.maximum, [jnp.max(part, axis=-1) for part in scores])
    total = reduce(jnp.add, [jnp.sum(jnp.exp(part - top[..., None]), axis=-1) for part in scores])
    output = jnp.zeros((tok_count, groups, group_ratio, head_size), jnp.float32)
    for distance in range(SPAN + 1):
        value_part = sources[distance][1]

        def compute_output(value_part=value_part, part=scores[distance]):
            probs_low = (jnp.exp(part - top[..., None]) / total[..., None]).astype(jnp.bfloat16)
            return jnp.einsum(
                "grqk,kgd->qgrd", probs_low, value_part, preferred_element_type=jnp.float32
            )

        output = output + compute_output()
    delta = jnp.transpose(jnp.sum(grad_group.astype(jnp.float32) * output, axis=-1), (1, 2, 0))
    query_total = jnp.zeros((tok_count, groups, group_ratio, head_size), jnp.float32)
    key_terms = []
    value_terms = []
    for distance in range(SPAN + 1):
        key_part, value_part = sources[distance]

        def compute_grads(key_part=key_part, value_part=value_part, part=scores[distance]):
            probs = jnp.exp(part - top[..., None]) / total[..., None]
            probs_low = probs.astype(jnp.bfloat16)
            dprobs = jnp.einsum(
                "qgrd,kgd->grqk", grad_group, value_part, preferred_element_type=jnp.float32
            )
            dscores = (probs * (dprobs - delta[..., None]) * scale).astype(jnp.bfloat16)
            query_term = jnp.einsum(
                "grqk,kgd->qgrd", dscores, key_part, preferred_element_type=jnp.float32
            )
            key_term = jnp.einsum(
                "grqk,qgrd->kgd", dscores, query_group, preferred_element_type=jnp.float32
            )
            value_term = jnp.einsum(
                "grqk,qgrd->kgd", probs_low, grad_group, preferred_element_type=jnp.float32
            )
            return (query_term, key_term, value_term)

        query_term, key_term, value_term = compute_grads()
        query_total = query_total + query_term
        key_terms.append(key_term)
        value_terms.append(value_term)
    key_total, value_total = (key_terms[0], value_terms[0])
    for distance in range(1, SPAN + 1):
        moved_key, moved_value = (
            passed_along(key_terms[distance].astype(jnp.bfloat16), "ctx", -distance).astype(
                jnp.float32
            ),
            passed_along(value_terms[distance].astype(jnp.bfloat16), "ctx", -distance).astype(
                jnp.float32
            ),
        )
        key_total = key_total + moved_key
        value_total = value_total + moved_value
    key_gradient, value_gradient = (
        lax.all_to_all(
            key_total.astype(jnp.bfloat16), "tp", split_axis=0, concat_axis=1, tiled=True
        ),
        lax.all_to_all(
            value_total.astype(jnp.bfloat16), "tp", split_axis=0, concat_axis=1, tiled=True
        ),
    )
    query_grads = query_total.reshape(tok_count, heads_local, head_size).astype(jnp.bfloat16)
    return (query_grads, key_gradient, value_gradient)


def solution(mesh):
    return jax.shard_map(
        on_device,
        mesh=mesh,
        in_specs=(
            P("ctx", "tp", None),
            P(("ctx", "tp"), None, None),
            P(("ctx", "tp"), None, None),
            P("ctx", "tp", None),
            P(),
        ),
        out_specs=(
            P("ctx", "tp", None),
            P(("ctx", "tp"), None, None),
            P(("ctx", "tp"), None, None),
        ),
        check_vma=False,
    )
```

profile of v0, /device:TPU:6, one launch (start us, length us, event | category | flops | bytes accessed | tf_op | source)
XLA Modules:
  0.0 101.3 jit_solution(3336469534919609904)
XLA Ops:
  0.6 1.6 %copy.138 = bf16[32,8,128]{2,0,1:T(8,128)(2,1)} copy(bf16[32,8,128]{2,1,0:T(8,128)(2,1)} %param.7) | data formatting | bytes 131072 | tf_op args[2]
  2.2 4.5 %all-to-all-start.1 = ((bf16[32,8,128]{2,0,1:T(8,128)(2,1)}), bf16[32,8,128]{2,0,1:T(8,128)(2,1)S(1)}, u32[]{:S(2)}, u32[]{:S(2)}) async-start(bf16[32,8,128]{2,0,1:T(8,128)(2,1)} %copy.138), calls=%async_computation.1 | async-start | bytes 131072 | tf_op jit(solution)/shard_map/all_to_all | solution.py:27
  6.7 0.7 copy.133
  7.7 1.5 %copy.134 = bf16[32,8,128]{2,0,1:T(8,128)(2,1)} copy(bf16[32,8,128]{2,1,0:T(8,128)(2,1)} %param.6) | data formatting | bytes 131072 | tf_op args[1]
  9.3 3.0 %all-to-all-done.1 = bf16[32,8,128]{2,0,1:T(8,128)(2,1)S(1)} async-done(((bf16[32,8,128]{2,0,1:T(8,128)(2,1)}), bf16[32,8,128]{2,0,1:T(8,128)(2,1)S(1)}, u32[]{:S(2)}, u32[]{:S(2)}) %all-to-all-start.1) | async-done | bytes 65568 | tf_op jit(solution)/shard_map/all_to_all | solution.py:27
  12.3 3.4 %all-to-all-start = ((bf16[32,8,128]{2,0,1:T(8,128)(2,1)}), bf16[32,8,128]{2,0,1:T(8,128)(2,1)S(1)}, u32[]{:S(2)}, u32[]{:S(2)}) async-start(bf16[32,8,128]{2,0,1:T(8,128)(2,1)} %copy.134), calls=%async_computation | async-start | bytes 131072 | tf_op jit(solution)/shard_map/all_to_all | solution.py:26
  15.7 0.5 and_and_fusion.1
  16.2 1.6 %copy.140 = bf16[256,16,128]{0,2,1:T(8,128)(2,1)S(1)} copy(bf16[256,16,128]{2,1,0:T(8,128)(2,1)} %param.8) | data formatting | bytes 2097152 | tf_op args[3]
  18.0 5.2 %collective-permute-start.3 = (bf16[256,1,128]{0,2,1:T(8,128)(2,1)S(1)}, bf16[256,1,128]{0,2,1:T(8,128)(2,1)S(1)}, u32[]{:S(2)}, u32[]{:S(2)}) collective-permute-start(bf16[256,1,128]{0,2,1:T(8,128)(2,1)S(1)} %copy.143), channel_id=1, source_target_pairs={{0,16},{8,24},{16,32},{24,40},{32,48},{40,56},{48,64},{56,72},{64,... | collective-permute-start | bytes 196616 | tf_op jit(solution)/shard_map/ppermute | solution.py:17
  23.2 3.8 %collective-permute-start.2 = (bf16[256,1,128]{0,2,1:T(8,128)(2,1)S(1)}, bf16[256,1,128]{0,2,1:T(8,128)(2,1)S(1)}, u32[]{:S(2)}, u32[]{:S(2)}) collective-permute-start(bf16[256,1,128]{0,2,1:T(8,128)(2,1)S(1)} %copy.143), channel_id=1, source_target_pairs={{0,8},{8,16},{16,24},{24,32},{32,40},{40,48},{48,56},{56,64},{64,7... | collective-permute-start | bytes 196616 | tf_op jit(solution)/shard_map/ppermute | solution.py:17
  27.0 6.4 %collective-permute-start.1 = (bf16[256,1,128]{2,0,1:T(8,128)(2,1)S(1)}, bf16[256,1,128]{2,0,1:T(8,128)(2,1)S(1)}, u32[]{:S(2)}, u32[]{:S(2)}) collective-permute-start(bf16[256,1,128]{2,0,1:T(8,128)(2,1)S(1)} %bitcast.322), channel_id=1, source_target_pairs={{0,16},{8,24},{16,32},{24,40},{32,48},{40,56},{48,64},{56,72},{64,... | collective-permute-start | bytes 196616 | tf_op jit(solution)/shard_map/ppermute | solution.py:17
  33.4 3.8 %collective-permute-start = (bf16[256,1,128]{2,0,1:T(8,128)(2,1)S(1)}, bf16[256,1,128]{2,0,1:T(8,128)(2,1)S(1)}, u32[]{:S(2)}, u32[]{:S(2)}) collective-permute-start(bf16[256,1,128]{2,0,1:T(8,128)(2,1)S(1)} %bitcast.323), channel_id=1, source_target_pairs={{0,8},{8,16},{16,24},{24,32},{32,40},{40,48},{48,56},{56,64},{64,7... | collective-permute-start | bytes 196616 | tf_op jit(solution)/shard_map/ppermute | solution.py:17
  37.3 0.9 fusion.15
  38.2 3.5 %collective-permute-done = bf16[256,1,128]{2,0,1:T(8,128)(2,1)S(1)} collective-permute-done((bf16[256,1,128]{2,0,1:T(8,128)(2,1)S(1)}, bf16[256,1,128]{2,0,1:T(8,128)(2,1)S(1)}, u32[]{:S(2)}, u32[]{:S(2)}) %collective-permute-start) | collective-permute-done | bytes 65568 | tf_op jit(solution)/shard_map/ppermute | solution.py:17
  41.7 0.9 fusion.16
  42.6 0.9 fusion.17
  43.5 2.8 %fusion.12 = (f32[16,256]{1,0:T(8,128)S(1)}, f32[16,256]{1,0:T(8,128)S(1)}, f32[16,256]{1,0:T(8,128)S(1)}) fusion(f32[256,256,16]{1,0,2:T(8,128)S(1)} %get-tuple-element.32, f32[16,256]{1,0:T(8,128)S(1)} %maximum_maximum_fusion, pred[256,256]{0,1:T(8,128)(4,1)S(1)} %get-tuple-element.24, f32[256,256,16]{1,0,2:T(8,128)S(1)} %get-tuple-element.28, ...), kind=kLoop, calls=%fused_computation.21 | loop fusion | flops 12570624 | bytes 12845056 | tf_op jit(solution)/shard_map/reduce_sum | solution.py:76
  46.3 1.1 %fusion.86 = bf16[256,1,128]{2,0,1:T(8,128)(2,1)S(1)} fusion(bf16[256,16,128]{0,2,1:T(8,128)(2,1)S(1)} %copy.140, f32[16,256]{1,0:T(8,128)S(1)} %add_add_fusion, f32[16,256]{1,0:T(8,128)S(1)} %maximum_maximum_fusion, f32[256,256,16]{1,0,2:T(8,128)S(1)} %get-tuple-element.28, pred[256,256]{0,1:T(8,128)(4,1)S(1)} %get-tuple-element.25), kind=kOutput, calls=%fused_computation.69 | convolution fusion | flops 273711104 | bytes 5406720 | tf_op jit(solution)/shard_map/grqk,qgrd->kgd/dot_general | solution.py:108
  47.5 1.1 %fusion.83 = bf16[256,1,128]{2,0,1:T(8,128)(2,1)S(1)} fusion(bf16[256,16,128]{0,2,1:T(8,128)(2,1)S(1)} %copy.140, f32[16,256]{1,0:T(8,128)S(1)} %add_add_fusion, f32[16,256]{1,0:T(8,128)S(1)} %maximum_maximum_fusion, f32[256,256,16]{1,0,2:T(8,128)S(1)} %get-tuple-element.32, pred[256,256]{0,1:T(8,128)(4,1)S(1)} %get-tuple-element.24), kind=kOutput, calls=%fused_computation.68 | convolution fusion | flops 273711104 | bytes 5406720 | tf_op jit(solution)/shard_map/grqk,qgrd->kgd/dot_general | solution.py:108
  48.6 2.0 %collective-permute-start.6 = (bf16[256,1,128]{2,0,1:T(8,128)(2,1)S(1)}, bf16[256,1,128]{2,0,1:T(8,128)(2,1)S(1)}, u32[]{:S(2)}, u32[]{:S(2)}) collective-permute-start(bf16[256,1,128]{2,0,1:T(8,128)(2,1)S(1)} %fusion.83), channel_id=1, source_target_pairs={{8,0},{16,8},{24,16},{32,24},{40,32},{48,40},{56,48},{64,56},{72,6... | collective-permute-start | bytes 196616 | tf_op jit(solution)/shard_map/ppermute | solution.py:17
  50.7 4.1 %collective-permute-start.7 = (bf16[256,1,128]{2,0,1:T(8,128)(2,1)S(1)}, bf16[256,1,128]{2,0,1:T(8,128)(2,1)S(1)}, u32[]{:S(2)}, u32[]{:S(2)}) collective-permute-start(bf16[256,1,128]{2,0,1:T(8,128)(2,1)S(1)} %fusion.86), channel_id=1, source_target_pairs={{16,0},{24,8},{32,16},{40,24},{48,32},{56,40},{64,48},{72,56},{80,... | collective-permute-start | bytes 196616 | tf_op jit(solution)/shard_map/ppermute | solution.py:17
  54.8 1.4 %fusion.41 = f32[16,256,128]{1,2,0:T(8,128)S(1)} fusion(bf16[256,128,1]{1,0,2:T(8,128)(2,1)S(1)} %bitcast.329, f32[16,256]{1,0:T(8,128)S(1)} %add_add_fusion, f32[16,256]{1,0:T(8,128)S(1)} %maximum_maximum_fusion, f32[256,256,16]{1,0,2:T(8,128)S(1)} %get-tuple-element.30, pred[256,256]{0,1:T(8,128)(4,1)S(1)} %get-tuple-element.26), kind=kOutput, calls=%fused_computation.51 | convolution fusion | flops 273678336 | bytes 6455296 | tf_op jit(solution)/shard_map/grqk,kgd->qgrd/dot_general | solution.py:83
  56.3 1.4 %fusion.37 = f32[16,256,128]{1,2,0:T(8,128)S(1)} fusion(bf16[256,1,128]{0,2,1:T(8,128)(2,1)S(1)} %collective-permute-done.2, f32[16,256]{1,0:T(8,128)S(1)} %add_add_fusion, f32[16,256]{1,0:T(8,128)S(1)} %maximum_maximum_fusion, f32[256,256,16]{1,0,2:T(8,128)S(1)} %get-tuple-element.32, pred[256,256]{0,1:T(8,128)(4,1)S(1)} %get-tuple-element.24), kind=kOutput, calls=%fused_computation.47 | convolution fusion | flops 273678336 | bytes 6455296 | tf_op jit(solution)/shard_map/grqk,kgd->qgrd/dot_general | solution.py:83
  57.7 1.6 %fusion.18 = f32[256,16]{0,1:T(8,128)S(1)} fusion(f32[16,256,128]{1,2,0:T(8,128)S(1)} %fusion.41, f32[16,256,128]{1,2,0:T(8,128)S(1)} %fusion.37, bf16[256,16,128]{0,2,1:T(8,128)(2,1)S(1)} %copy.140, bf16[256,1,128]{0,2,1:T(8,128)(2,1)S(1)} %collective-permute-done.3, f32[16,256]{1,0:T(8,128)S(1)} %add_add_fusion, f32[16,256]{1,0:T(8,128)S(1)} %maximum_maximum_fusion, ...), kind=kOutput, calls=%fused_computation.28 | convolution fusion | flops 276295680 | bytes 9617408 | tf_op jit(solution)/shard_map/grqk,kgd->qgrd/dot_general | solution.py:83
  59.3 1.7 %fusion.8 = bf16[1,16,256,256]{2,3,1,0:T(8,128)(2,1)S(1)} fusion(bf16[256,128,1]{1,0,2:T(8,128)(2,1)S(1)} %bitcast.330, bf16[256,16,128]{0,2,1:T(8,128)(2,1)S(1)} %copy.140, f32[16,256]{1,0:T(8,128)S(1)} %bitcast.332, f32[16,256]{1,0:T(8,128)S(1)} %add_add_fusion, f32[16,256]{1,0:T(8,128)S(1)} %maximum_maximum_fusion, ...), kind=kOutput, calls=%fused_computation.11 | convolution fusion | flops 276824064 | bytes 7520256 | tf_op jit(solution)/shard_map/qgrd,kgd->grqk/dot_general | solution.py:98
  61.0 1.7 %fusion.2 = bf16[1,16,256,256]{2,3,1,0:T(8,128)(2,1)S(1)} fusion(bf16[256,16,128]{0,2,1:T(8,128)(2,1)S(1)} %copy.140, f32[16,256]{1,0:T(8,128)S(1)} %bitcast.333, f32[16,256]{1,0:T(8,128)S(1)} %add_add_fusion, f32[16,256]{1,0:T(8,128)S(1)} %maximum_maximum_fusion, f32[256,256,16]{1,0,2:T(8,128)S(1)} %get-tuple-element.28, ...), kind=kOutput, calls=%fused_computation.3 | convolution fusion | flops 276824064 | bytes 7520256 | tf_op jit(solution)/shard_map/qgrd,kgd->grqk/dot_general | solution.py:98
  62.7 0.7 fusion.92
  63.5 1.7 %fusion.5 = bf16[1,16,256,256]{2,3,1,0:T(8,128)(2,1)S(1)} fusion(bf16[256,16,128]{0,2,1:T(8,128)(2,1)S(1)} %copy.140, f32[16,256]{1,0:T(8,128)S(1)} %bitcast.334, f32[16,256]{1,0:T(8,128)S(1)} %add_add_fusion, f32[16,256]{1,0:T(8,128)S(1)} %maximum_maximum_fusion, f32[256,256,16]{1,0,2:T(8,128)S(1)} %get-tuple-element.32, ...), kind=kOutput, calls=%fused_computation.7 | convolution fusion | flops 276824064 | bytes 7520256 | tf_op jit(solution)/shard_map/qgrd,kgd->grqk/dot_general | solution.py:98
  65.2 1.4 %fusion.89 = bf16[256,1,128]{2,0,1:T(8,128)(2,1)} fusion(bf16[1,16,256,256]{2,3,1,0:T(8,128)(2,1)S(1)} %fusion.5, bf16[256,16,128]{2,1,0:T(8,128)(2,1)S(1)} %copy-done), kind=kOutput, calls=%fused_computation.70 | convolution fusion | flops 268468224 | bytes 3211264 | tf_op jit(solution)/shard_map/grqk,qgrd->kgd/dot_general | solution.py:105
  66.6 4.4 %collective-permute-start.4 = (bf16[256,1,128]{2,0,1:T(8,128)(2,1)}, bf16[256,1,128]{2,0,1:T(8,128)(2,1)S(1)}, u32[]{:S(2)}, u32[]{:S(2)}) collective-permute-start(bf16[256,1,128]{2,0,1:T(8,128)(2,1)} %fusion.89), channel_id=1, source_target_pairs={{8,0},{16,8},{24,16},{32,24},{40,32},{48,40},{56,48},{64,56},{72,6... | collective-permute-start | bytes 196616 | tf_op jit(solution)/shard_map/ppermute | solution.py:17
  71.0 4.4 %collective-permute-start.5 = (bf16[256,1,128]{2,0,1:T(8,128)(2,1)S(1)}, bf16[256,1,128]{2,0,1:T(8,128)(2,1)S(1)}, u32[]{:S(2)}, u32[]{:S(2)}) collective-permute-start(bf16[256,1,128]{2,0,1:T(8,128)(2,1)S(1)} %fusion.92), channel_id=1, source_target_pairs={{16,0},{24,8},{32,16},{40,24},{48,32},{56,40},{64,48},{72,56},{80,... | collective-permute-start | bytes 196616 | tf_op jit(solution)/shard_map/ppermute | solution.py:17
  75.5 0.8 fusion.29
  76.2 2.1 %fusion.25 = f32[16,256,128]{2,1,0:T(8,128)} fusion(bf16[1,16,256,256]{2,3,1,0:T(8,128)(2,1)S(1)} %fusion.5, bf16[256,1,128]{2,0,1:T(8,128)(2,1)S(1)} %collective-permute-done), kind=kOutput, calls=%fused_computation.35 | convolution fusion | flops 268435456 | bytes 4259840 | tf_op jit(solution)/shard_map/grqk,kgd->qgrd/dot_general | solution.py:102
  78.3 1.2 %add_convert_fusion.1 = bf16[256,1,128]{2,0,1:T(8,128)(2,1)S(1)} fusion(bf16[256,1,128]{2,0,1:T(8,128)(2,1)S(1)} %collective-permute-done.7, bf16[256,1,128]{2,0,1:T(8,128)(2,1)S(1)} %collective-permute-done.6, bf16[256,16,128]{0,2,1:T(8,128)(2,1)S(1)} %copy-done.4, f32[16,256]{1,0:T(8,128)S(1)} %add_add_fusion, f32[16,256]{1,0:T(8,128)S(1)} %maximum_maximum_fusion, ...), kind=kOutput, calls=%fused_computation.84 | convolution fusion | flops 273842176 | bytes 5537792 | tf_op jit(solution)/shard_map/grqk,qgrd->kgd/dot_general | solution.py:108
  79.5 0.5 broadcast.399
  80.0 0.7 reduce.9
  80.7 0.6 reshape.515
  81.4 4.7 %all-to-all-start.3 = ((bf16[8,2,2048]{2,1,0:T(2,128)(2,1)}), bf16[8,2,2048]{2,1,0:T(2,128)(2,1)S(1)}, u32[]{:S(2)}, u32[]{:S(2)}) async-start(bf16[8,2,2048]{2,1,0:T(2,128)(2,1)} %reshape.515), calls=%async_computation.3 | async-start | bytes 131072 | tf_op jit(solution)/shard_map/all_to_all | solution.py:133
  86.1 2.3 %add_convert_fusion.2 = bf16[256,1,128]{2,0,1:T(8,128)(2,1)S(1)} fusion(bf16[256,1,128]{2,0,1:T(8,128)(2,1)S(1)} %collective-permute-done.5, bf16[256,1,128]{2,0,1:T(8,128)(2,1)S(1)} %collective-permute-done.4, bf16[256,16,128]{2,1,0:T(8,128)(2,1)S(1)} %copy-done, bf16[1,16,256,256]{2,3,1,0:T(8,128)(2,1)} %copy-done.2), kind=kOutput, calls=%fused_computation.85 | convolution fusion | flops 268599296 | bytes 3342336 | tf_op jit(solution)/shard_map/grqk,qgrd->kgd/dot_general | solution.py:105
  88.4 0.7 reduce.8
  89.1 0.6 reshape.513
  89.7 1.9 %all-to-all-done.3 = bf16[8,2,2048]{2,1,0:T(2,128)(2,1)S(1)} async-done(((bf16[8,2,2048]{2,1,0:T(2,128)(2,1)}), bf16[8,2,2048]{2,1,0:T(2,128)(2,1)S(1)}, u32[]{:S(2)}, u32[]{:S(2)}) %all-to-all-start.3) | async-done | bytes 65568 | tf_op jit(solution)/shard_map/all_to_all | solution.py:133
  91.7 3.4 %all-to-all-start.2 = ((bf16[8,2,2048]{2,1,0:T(2,128)(2,1)}), bf16[8,2,2048]{2,1,0:T(2,128)(2,1)S(1)}, u32[]{:S(2)}, u32[]{:S(2)}) async-start(bf16[8,2,2048]{2,1,0:T(2,128)(2,1)} %reshape.513), calls=%async_computation.2 | async-start | bytes 131072 | tf_op jit(solution)/shard_map/all_to_all | solution.py:130
  95.0 3.0 %fusion.50 = bf16[256,16,128]{2,0,1:T(8,128)(2,1)S(1)} fusion(bf16[1,16,256,256]{2,3,1,0:T(8,128)(2,1)} %copy-done.1, f32[16,256,128]{2,1,0:T(8,128)S(1)} %fusion.29, f32[16,256,128]{2,1,0:T(8,128)} %fusion.25, bf16[256,1,128]{2,0,1:T(8,128)(2,1)S(1)} %collective-permute-done.1), kind=kOutput, calls=%fused_computation.57 | convolution fusion | flops 270008320 | bytes 7405568 | tf_op jit(solution)/shard_map/grqk,kgd->qgrd/dot_general | solution.py:102
  98.0 1.6 %copy.162 = bf16[256,16,128]{2,1,0:T(8,128)(2,1)} copy(bf16[256,16,128]{2,0,1:T(8,128)(2,1)S(1)} %fusion.50) | data formatting | bytes 2097152
  99.8 0.7 copy.164
  100.4 0.2 all-to-all-done.2
  100.6 0.7 copy.163
  (33 shorter events, 0.7 us)
Async XLA Ops:
  0.6 36.6 %copy-start = (bf16[256,16,128]{2,1,0:T(8,128)(2,1)S(1)}, bf16[256,16,128]{2,1,0:T(8,128)(2,1)}, u32[]{:S(2)}) copy-start(bf16[256,16,128]{2,1,0:T(8,128)(2,1)} %param.5) | copy-start | bytes 3145732
  2.2 10.1 %all-to-all-start.1 = ((bf16[32,8,128]{2,0,1:T(8,128)(2,1)}), bf16[32,8,128]{2,0,1:T(8,128)(2,1)S(1)}, u32[]{:S(2)}, u32[]{:S(2)}) async-start(bf16[32,8,128]{2,0,1:T(8,128)(2,1)} %copy.138), calls=%async_computation.1 | async-start | bytes 131072 | tf_op jit(solution)/shard_map/all_to_all | solution.py:27
  12.3 14.7 %all-to-all-start = ((bf16[32,8,128]{2,0,1:T(8,128)(2,1)}), bf16[32,8,128]{2,0,1:T(8,128)(2,1)S(1)}, u32[]{:S(2)}, u32[]{:S(2)}) async-start(bf16[32,8,128]{2,0,1:T(8,128)(2,1)} %copy.134), calls=%async_computation | async-start | bytes 131072 | tf_op jit(solution)/shard_map/all_to_all | solution.py:26
  17.9 45.6 %copy-start.3 = (bf16[256,16,128]{0,2,1:T(8,128)(2,1)}, bf16[256,16,128]{0,2,1:T(8,128)(2,1)S(1)}, u32[]{:S(2)}) copy-start(bf16[256,16,128]{0,2,1:T(8,128)(2,1)S(1)} %copy.140) | copy-start | bytes 3145732
  18.0 39.7 %collective-permute-start.3 = (bf16[256,1,128]{0,2,1:T(8,128)(2,1)S(1)}, bf16[256,1,128]{0,2,1:T(8,128)(2,1)S(1)}, u32[]{:S(2)}, u32[]{:S(2)}) collective-permute-start(bf16[256,1,128]{0,2,1:T(8,128)(2,1)S(1)} %copy.143), channel_id=1, source_target_pairs={{0,16},{8,24},{16,32},{24,40},{32,48},{40,56},{48,64},{56,72},{64,... | collective-permute-start | bytes 196616 | tf_op jit(solution)/shard_map/ppermute | solution.py:17
  23.2 33.1 %collective-permute-start.2 = (bf16[256,1,128]{0,2,1:T(8,128)(2,1)S(1)}, bf16[256,1,128]{0,2,1:T(8,128)(2,1)S(1)}, u32[]{:S(2)}, u32[]{:S(2)}) collective-permute-start(bf16[256,1,128]{0,2,1:T(8,128)(2,1)S(1)} %copy.143), channel_id=1, source_target_pairs={{0,8},{8,16},{16,24},{24,32},{32,40},{40,48},{48,56},{56,64},{64,7... | collective-permute-start | bytes 196616 | tf_op jit(solution)/shard_map/ppermute | solution.py:17
  27.0 15.6 %collective-permute-start.1 = (bf16[256,1,128]{2,0,1:T(8,128)(2,1)S(1)}, bf16[256,1,128]{2,0,1:T(8,128)(2,1)S(1)}, u32[]{:S(2)}, u32[]{:S(2)}) collective-permute-start(bf16[256,1,128]{2,0,1:T(8,128)(2,1)S(1)} %bitcast.322), channel_id=1, source_target_pairs={{0,16},{8,24},{16,32},{24,40},{32,48},{40,56},{48,64},{56,72},{64,... | collective-permute-start | bytes 196616 | tf_op jit(solution)/shard_map/ppermute | solution.py:17
  33.4 8.3 %collective-permute-start = (bf16[256,1,128]{2,0,1:T(8,128)(2,1)S(1)}, bf16[256,1,128]{2,0,1:T(8,128)(2,1)S(1)}, u32[]{:S(2)}, u32[]{:S(2)}) collective-permute-start(bf16[256,1,128]{2,0,1:T(8,128)(2,1)S(1)} %bitcast.323), channel_id=1, source_target_pairs={{0,8},{8,16},{16,24},{24,32},{32,40},{40,48},{48,56},{56,64},{64,7... | collective-permute-start | bytes 196616 | tf_op jit(solution)/shard_map/ppermute | solution.py:17
  48.6 29.6 %collective-permute-start.6 = (bf16[256,1,128]{2,0,1:T(8,128)(2,1)S(1)}, bf16[256,1,128]{2,0,1:T(8,128)(2,1)S(1)}, u32[]{:S(2)}, u32[]{:S(2)}) collective-permute-start(bf16[256,1,128]{2,0,1:T(8,128)(2,1)S(1)} %fusion.83), channel_id=1, source_target_pairs={{8,0},{16,8},{24,16},{32,24},{40,32},{48,40},{56,48},{64,56},{72,6... | collective-permute-start | bytes 196616 | tf_op jit(solution)/shard_map/ppermute | solution.py:17
  50.7 27.6 %collective-permute-start.7 = (bf16[256,1,128]{2,0,1:T(8,128)(2,1)S(1)}, bf16[256,1,128]{2,0,1:T(8,128)(2,1)S(1)}, u32[]{:S(2)}, u32[]{:S(2)}) collective-permute-start(bf16[256,1,128]{2,0,1:T(8,128)(2,1)S(1)} %fusion.86), channel_id=1, source_target_pairs={{16,0},{24,8},{32,16},{40,24},{48,32},{56,40},{64,48},{72,56},{80,... | collective-permute-start | bytes 196616 | tf_op jit(solution)/shard_map/ppermute | solution.py:17
  61.0 14.5 %copy-start.2 = (bf16[1,16,256,256]{2,3,1,0:T(8,128)(2,1)}, bf16[1,16,256,256]{2,3,1,0:T(8,128)(2,1)S(1)}, u32[]{:S(2)}) copy-start(bf16[1,16,256,256]{2,3,1,0:T(8,128)(2,1)S(1)} %fusion.8) | copy-start | bytes 6291460
  62.7 2.5 %copy-start.1 = (bf16[1,16,256,256]{2,3,1,0:T(8,128)(2,1)}, bf16[1,16,256,256]{2,3,1,0:T(8,128)(2,1)S(1)}, u32[]{:S(2)}) copy-start(bf16[1,16,256,256]{2,3,1,0:T(8,128)(2,1)S(1)} %fusion.2) | copy-start | bytes 6291460
  66.6 11.7 %copy-start.4 = (bf16[256,16,128]{0,2,1:T(8,128)(2,1)S(1)}, bf16[256,16,128]{0,2,1:T(8,128)(2,1)}, u32[]{:S(2)}) copy-start(bf16[256,16,128]{0,2,1:T(8,128)(2,1)} %copy-done.3) | copy-start | bytes 3145732
  66.6 19.5 %collective-permute-start.4 = (bf16[256,1,128]{2,0,1:T(8,128)(2,1)}, bf16[256,1,128]{2,0,1:T(8,128)(2,1)S(1)}, u32[]{:S(2)}, u32[]{:S(2)}) collective-permute-start(bf16[256,1,128]{2,0,1:T(8,128)(2,1)} %fusion.89), channel_id=1, source_target_pairs={{8,0},{16,8},{24,16},{32,24},{40,32},{48,40},{56,48},{64,56},{72,6... | collective-permute-start | bytes 196616 | tf_op jit(solution)/shard_map/ppermute | solution.py:17
  71.0 15.0 %collective-permute-start.5 = (bf16[256,1,128]{2,0,1:T(8,128)(2,1)S(1)}, bf16[256,1,128]{2,0,1:T(8,128)(2,1)S(1)}, u32[]{:S(2)}, u32[]{:S(2)}) collective-permute-start(bf16[256,1,128]{2,0,1:T(8,128)(2,1)S(1)} %fusion.92), channel_id=1, source_target_pairs={{16,0},{24,8},{32,16},{40,24},{48,32},{56,40},{64,48},{72,56},{80,... | collective-permute-start | bytes 196616 | tf_op jit(solution)/shard_map/ppermute | solution.py:17
  81.4 10.3 %all-to-all-start.3 = ((bf16[8,2,2048]{2,1,0:T(2,128)(2,1)}), bf16[8,2,2048]{2,1,0:T(2,128)(2,1)S(1)}, u32[]{:S(2)}, u32[]{:S(2)}) async-start(bf16[8,2,2048]{2,1,0:T(2,128)(2,1)} %reshape.515), calls=%async_computation.3 | async-start | bytes 131072 | tf_op jit(solution)/shard_map/all_to_all | solution.py:133
  91.7 8.9 %all-to-all-start.2 = ((bf16[8,2,2048]{2,1,0:T(2,128)(2,1)}), bf16[8,2,2048]{2,1,0:T(2,128)(2,1)S(1)}, u32[]{:S(2)}, u32[]{:S(2)}) async-start(bf16[8,2,2048]{2,1,0:T(2,128)(2,1)} %reshape.513), calls=%async_computation.2 | async-start | bytes 131072 | tf_op jit(solution)/shard_map/all_to_all | solution.py:130
where the time goes:
time: 103 us; the launch traced here: 101 us
  starting transfers between devices  50.1 us (49%)
  matrix products  26 us (25%)
  local copies, waits for them, and re-layouts  10.5 us (10%)
  waiting for transfers between devices  8.64 us (8%)
  other arithmetic  5.02 us (5%)
  between operations  1.04 us (1%)
    ppermute x8, starting transfers between devices, passed_along(): return lax.ppermute(block, axis, route)  34.2 us
    unnamed x22, local copies, waits for them, and re-layouts  9.13 us
    dot_general x3, matrix products, compute_grads(): jnp.einsum('grqk,kgd->qgrd', dscores, key_part, preferred_element_type=jn...  5.81 us
    dot_general x3, matrix products, compute_grads(): jnp.einsum('qgrd,kgd->grqk', grad_group, value_part, preferred_element_ty...  5.1 us
    all_to_all x1, starting transfers between devices, on_device(): lax.all_to_all(value_total.astype(jnp.bfloat16), 'tp', split_axis=0, conc...  4.68 us
    all_to_all x1, starting transfers between devices, on_device(): lax.all_to_all(values, 'tp', split_axis=1, concat_axis=0, tiled=True)  4.47 us
    dot_general x3, matrix products, compute_output(): jnp.einsum('grqk,kgd->qgrd', probs_low, value_part, preferred_element_typ...  4.45 us
    dot_general x3, matrix products, compute_grads(): jnp.einsum('grqk,qgrd->kgd', dscores, query_group, preferred_element_type...  4.44 us
  transfers between devices with their start and end apart: 12, of which 4 were waited for; matrix products, arithmetic and copies ran while one was open for 39% of the time, Pallas kernels for 0%

commit v1 on v0

v1 whole, which is shorter than its diff:
```python
import functools
import math

import jax
import jax.numpy as jnp
from jax import lax
from jax.experimental import pallas as pl
from jax.experimental.pallas import tpu as pltpu
from jax.sharding import PartitionSpec as P

BLK = 128
BLK_DEV = 2
BACK = 4
LOG2E = math.log2(math.e)
LOW = -3.0e38
OFF = 1.0e30

VMEM = pl.BlockSpec(memory_space=pltpu.VMEM)
SMEM = pl.BlockSpec(memory_space=pltpu.SMEM)


def passed_along(block, axis, distance):
    devices = range(lax.axis_size(axis))
    route = [(i - distance, i) for i in devices if i - distance in devices]
    return lax.ppermute(block, axis, route)


def to_groups(k_ref, v_ref, out_ref, wide):
    for which, ref in enumerate((k_ref, v_ref)):
        wide[...] = ref[...].astype(jnp.float32)
        for g in range(wide.shape[1]):
            out_ref[g, which] = wide[:, g, :].astype(out_ref.dtype)


def from_groups(in_ref, k_ref, v_ref, wide):
    for which, ref in enumerate((k_ref, v_ref)):
        for g in range(wide.shape[1]):
            wide[:, g, :] = in_ref[g, which].astype(jnp.float32)
        ref[...] = wide[...].astype(ref.dtype)


def attention(prev_ref, q_ref, g_ref, x0_ref, x1_ref, x2_ref,
              dq_ref, y0_ref, y1_ref, y2_ref,
              kk, vv, kt, dk, dv, *, heads):
    step = pl.program_id(0)
    steps = pl.num_programs(0)
    head_size = q_ref.shape[1]
    rows = q_ref.shape[0]
    span = (BACK + 1) * BLK
    scale = 1.0 / math.sqrt(head_size)
    factor = scale * LOG2E
    local = BLK_DEV * BLK
    f32 = jnp.float32

    @pl.when(step == 0)
    def _():
        for i, ref in enumerate((x2_ref, x1_ref, x0_ref)):
            k = ref[:, 0].reshape(local, head_size)
            kk[pl.ds(i * local, local), :] = k
            vv[pl.ds(i * local, local), :] = ref[:, 1].reshape(local, head_size)
            kt[:, pl.ds(i * local, local)] = k.astype(f32).T.astype(kk.dtype)
        dk[...] = jnp.zeros_like(dk)
        dv[...] = jnp.zeros_like(dv)

    half = steps // BLK_DEV

    def work(block):
        base = block * BLK
        prev = prev_ref[block]
        window = pl.ds(base, span)
        q = q_ref[...]
        g = g_ref[...]
        nt = (((1,), (1,)), ((), ()))
        st = lax.dot_general(kk[window, :], q, nt, preferred_element_type=f32)
        dpt = lax.dot_general(vv[window, :], g, nt, preferred_element_type=f32)
        first_row = (step - block * half) * rows
        key = lax.broadcasted_iota(jnp.int32, (BLK, rows), 0) * heads
        row = lax.broadcasted_iota(jnp.int32, (BLK, rows), 1) + first_row
        parts = [st[o * BLK:(o + 1) * BLK] for o in range(BACK + 1)]
        parts[BACK] = jnp.where(key <= row, parts[BACK], -OFF)
        off = [jnp.where(prev >= BACK - o, 0.0, OFF).astype(f32) for o in range(BACK)] + [None]
        top = jnp.max(parts[BACK], axis=0, keepdims=True)
        for o in range(BACK):
            top = jnp.maximum(top, jnp.max(parts[o], axis=0, keepdims=True) - off[o])
        low = top * factor
        total = jnp.zeros((1, rows), f32)
        es = []
        for o in range(BACK + 1):
            shift = low if off[o] is None else low + off[o]
            e = jnp.exp2(parts[o] * factor - shift)
            total = total + jnp.sum(e, axis=0, keepdims=True)
            es.append(e)
        inv = 1.0 / total
        delta = jnp.zeros((1, rows), f32)
        fs, ps, ds = [], [], []
        for o in range(BACK + 1):
            p = es[o] * inv
            p_round = p.astype(kk.dtype)
            d = dpt[o * BLK:(o + 1) * BLK]
            delta = delta + jnp.sum(p_round.astype(f32) * d, axis=0, keepdims=True)
            fs.append(p)
            ps.append(p_round)
        for o in range(BACK + 1):
            d = dpt[o * BLK:(o + 1) * BLK]
            ds.append((fs[o] * (d - delta) * scale).astype(kk.dtype))
        p_low = jnp.concatenate(ps, axis=0)
        d_low = jnp.concatenate(ds, axis=0)
        dv[window, :] += jnp.dot(p_low, g, preferred_element_type=f32)
        dk[window, :] += jnp.dot(d_low, q, preferred_element_type=f32)
        dqt = jnp.dot(kt[:, window], d_low, preferred_element_type=f32)
        dq_ref[...] = dqt.T.astype(dq_ref.dtype)

    for block in range(BLK_DEV):
        pl.when(step // half == block)(functools.partial(work, block))

    @pl.when(step == steps - 1)
    def _():
        for i, ref in enumerate((y2_ref, y1_ref, y0_ref)):
            k = dk[pl.ds(i * local, local), :]
            v = dv[pl.ds(i * local, local), :]
            ref[:, 0] = k.astype(ref.dtype).reshape(ref.shape[0], -1, head_size)
            ref[:, 1] = v.astype(ref.dtype).reshape(ref.shape[0], -1, head_size)


def local_grads(prev, q, g, x0, x1, x2, heads, rows=512):
    total_rows, head_size = q.shape
    steps = total_rows // rows
    keys = 3 * BLK_DEV * BLK
    row_spec = pl.BlockSpec((rows, head_size), lambda i: (i, 0))
    low = q.dtype
    return pl.pallas_call(
        functools.partial(attention, heads=heads),
        grid=(steps,),
        out_shape=(
            jax.ShapeDtypeStruct(q.shape, low),
            jax.ShapeDtypeStruct(x0.shape, low),
            jax.ShapeDtypeStruct(x0.shape, low),
            jax.ShapeDtypeStruct(x0.shape, low),
        ),
        in_specs=[SMEM, row_spec, row_spec, VMEM, VMEM, VMEM],
        out_specs=(row_spec, VMEM, VMEM, VMEM),
        scratch_shapes=[
            pltpu.VMEM((keys, head_size), low),
            pltpu.VMEM((keys, head_size), low),
            pltpu.VMEM((head_size, keys), low),
            pltpu.VMEM((keys, head_size), jnp.float32),
            pltpu.VMEM((keys, head_size), jnp.float32),
        ],
        compiler_params=pltpu.CompilerParams(
            dimension_semantics=("arbitrary",), vmem_limit_bytes=48 << 20
        ),
        name="local_grads",
    )(prev, q, g, x0, x1, x2)


def on_device(queries, keys, values, output_gradient, doc_blocks):
    tok_count, heads, head_size = queries.shape
    tok_part, groups, _ = keys.shape
    low = queries.dtype
    packed = pl.pallas_call(
        to_groups,
        out_shape=jax.ShapeDtypeStruct((groups, 2, tok_part, head_size), low),
        in_specs=[VMEM, VMEM],
        out_specs=VMEM,
        scratch_shapes=[pltpu.VMEM(keys.shape, jnp.float32)],
        name="to_groups",
    )(keys, values)
    x0 = lax.all_to_all(packed, "tp", split_axis=0, concat_axis=0, tiled=True)
    x1 = passed_along(x0, "ctx", 1)
    x2 = passed_along(x0, "ctx", 2)
    docs = doc_blocks.shape[0]
    upto = jnp.arange(docs)[:, None] >= jnp.arange(docs)[None, :]
    ends = jnp.sum(jnp.where(upto, doc_blocks[None, :], 0), axis=1)
    mine = lax.axis_index("ctx") * BLK_DEV + jnp.arange(BLK_DEV, dtype=jnp.int32)
    start = jnp.max(jnp.where(ends[None, :] <= mine[:, None], ends[None, :], 0), axis=1)
    prev = (mine - start).astype(jnp.int32)
    dq, y0, y1, y2 = local_grads(
        prev,
        queries.reshape(tok_count * heads, head_size),
        output_gradient.reshape(tok_count * heads, head_size),
        x0, x1, x2, heads,
    )
    r2 = passed_along(y2, "ctx", -2)
    r1 = passed_along(y1, "ctx", -1)
    f32 = jnp.float32
    summed = (y0.astype(f32) + r1.astype(f32) + r2.astype(f32)).astype(low)
    back = lax.all_to_all(summed, "tp", split_axis=0, concat_axis=0, tiled=True)
    key_gradient, value_gradient = pl.pallas_call(
        from_groups,
        out_shape=(
            jax.ShapeDtypeStruct(keys.shape, low),
            jax.ShapeDtypeStruct(values.shape, low),
        ),
        in_specs=[VMEM],
        out_specs=(VMEM, VMEM),
        scratch_shapes=[pltpu.VMEM(keys.shape, jnp.float32)],
        name="from_groups",
    )(back)
    return dq.reshape(queries.shape), key_gradient, value_gradient


def solution(mesh):
    return jax.shard_map(
        on_device,
        mesh=mesh,
        in_specs=(
            P("ctx", "tp", None),
            P(("ctx", "tp"), None, None),
            P(("ctx", "tp"), None, None),
            P("ctx", "tp", None),
            P(),
        ),
        out_specs=(
            P("ctx", "tp", None),
            P(("ctx", "tp"), None, None),
            P(("ctx", "tp"), None, None),
        ),
        check_vma=False,
    )
```

time: 103 us -> 73.9 us (0.72); the launches traced: 101 us -> 73.5 us
  starting transfers between devices: 50.1 us -> 21 us
  matrix products: 26 us -> 0 us
  Pallas kernels: 0 us -> 17.3 us
  waiting for transfers between devices: 8.64 us -> 21.9 us
  blocking collectives: 0 us -> 9.16 us
  local copies, waits for them, and re-layouts: 10.5 us -> 3.1 us
  other arithmetic: 5.02 us -> 0.36 us
    dot_general x18 -> x0, matrix products: 26 us -> none  [the longest x3 5.81 us: compute_grads(): jnp.einsum('grqk,kgd->qgrd', dscores, key_part, preferred_element_type=jn...]
    ppermute x8 -> x4, starting transfers between devices: 34.2 us -> 16.5 us  [passed_along(): return lax.ppermute(block, axis, route)]
    pallas_call x0 -> x3, Pallas kernels: none -> 17.3 us  [the longest x1 13.8 us: local_grads(): pl.pallas_call(functools.partial(attention, heads=heads), grid=(steps,),...]
    ppermute x8 -> x4, waiting for transfers between devices: 3.53 us -> 16.8 us  [passed_along(): return lax.ppermute(block, axis, route)]
    all_to_all x4 -> x1, starting transfers between devices: 15.9 us -> 4.47 us  [on_device(): x0 = lax.all_to_all(packed, 'tp', split_axis=0, concat_axis=0, tiled=True)]
    all_to_all x0 -> x1, blocking collectives: none -> 9.16 us  [on_device(): back = lax.all_to_all(summed, 'tp', split_axis=0, concat_axis=0, tiled=True)]
    unnamed x22 -> x6, local copies, waits for them, and re-layouts: 9.13 us -> 3.1 us
    reduce_sum x2 -> x1, other arithmetic: 2.89 us -> 0.11 us  [on_device(): ends = jnp.sum(jnp.where(upto, doc_blocks[None, :], 0), axis=1)]
  transfers between devices with their start and end apart: 12 -> 5, of which waited for: 4 -> 4; matrix products, arithmetic and copies ran while one was open for 39% -> 0% of each run, Pallas kernels for 0% -> 0%
where the time goes in v1:
time: 73.9 us; the launch traced here: 73.5 us
  waiting for transfers between devices  21.9 us (30%)
  starting transfers between devices  21 us (28%)
  Pallas kernels  17.3 us (23%)
  blocking collectives  9.16 us (12%)
  local copies, waits for them, and re-layouts  3.1 us (4%)
    ppermute x4, waiting for transfers between devices, passed_along(): return lax.ppermute(block, axis, route)  16.8 us
    ppermute x4, starting transfers between devices, passed_along(): return lax.ppermute(block, axis, route)  16.5 us
    pallas_call x1, Pallas kernels, local_grads(): pl.pallas_call(functools.partial(attention, heads=heads), grid=(steps,),...  13.8 us
    all_to_all x1, blocking collectives, on_device(): back = lax.all_to_all(summed, 'tp', split_axis=0, concat_axis=0, tiled=True)  9.16 us
    all_to_all x1, waiting for transfers between devices, on_device(): x0 = lax.all_to_all(packed, 'tp', split_axis=0, concat_axis=0, tiled=True)  5.14 us
    all_to_all x1, starting transfers between devices, on_device(): x0 = lax.all_to_all(packed, 'tp', split_axis=0, concat_axis=0, tiled=True)  4.47 us
    unnamed x6, local copies, waits for them, and re-layouts  3.1 us
    pallas_call x1, Pallas kernels, on_device(): pl.pallas_call(to_groups, out_shape=jax.ShapeDtypeStruct((groups, 2, tok_...  1.81 us
  transfers between devices with their start and end apart: 5, of which 4 were waited for; matrix products, arithmetic and copies ran while one was open for 0% of the time, Pallas kernels for 0%

profile of v1, /device:TPU:6, one launch (start us, length us, event | category | flops | bytes accessed | tf_op | source)
XLA Modules:
  0.0 73.5 jit_solution(13349260921677462776)
XLA Ops:
  0.6 1.8 %to_groups.1 = bf16[8,2,32,128]{3,2,1,0:T(8,128)(2,1)} custom-call(bf16[32,8,128]{2,1,0:T(8,128)(2,1)} %k_ref.1, bf16[32,8,128]{2,1,0:T(8,128)(2,1)} %v_ref.1), custom_call_target="tpu_custom_call" | custom-call | tf_op jit(solution)/shard_map/to_groups/pallas_call | solution.py:160
  2.4 4.5 %all-to-all-start = ((bf16[8,2,32,128]{3,2,1,0:T(8,128)(2,1)}), bf16[8,2,32,128]{3,2,1,0:T(8,128)(2,1)S(1)}, u32[]{:S(2)}, u32[]{:S(2)}) async-start(bf16[8,2,32,128]{3,2,1,0:T(8,128)(2,1)} %to_groups.1), calls=%async_computation | async-start | bytes 262144 | tf_op jit(solution)/shard_map/all_to_all | solution.py:168
  6.9 0.0 copy-start.2
  6.9 0.7 copy-done.2
  7.6 0.1 select_reduce_fusion
  7.7 0.2 fusion
  7.9 5.1 %all-to-all-done.x0_ref = bf16[8,2,32,128]{3,2,1,0:T(8,128)(2,1)S(1)} async-done(((bf16[8,2,32,128]{3,2,1,0:T(8,128)(2,1)}), bf16[8,2,32,128]{3,2,1,0:T(8,128)(2,1)S(1)}, u32[]{:S(2)}, u32[]{:S(2)}) %all-to-all-start) | async-done | bytes 131104 | tf_op jit(solution)/shard_map/all_to_all | solution.py:168
  13.0 5.2 %collective-permute-start.1 = (bf16[8,2,32,128]{3,2,1,0:T(8,128)(2,1)S(1)}, bf16[8,2,32,128]{3,2,1,0:T(8,128)(2,1)S(1)}, u32[]{:S(2)}, u32[]{:S(2)}) collective-permute-start(bf16[8,2,32,128]{3,2,1,0:T(8,128)(2,1)S(1)} %all-to-all-done.x0_ref), channel_id=1, source_target_pairs={{0,16},{8,24},{16,32},{24,40},{32,48},{40,56},{48,64},{56,72},{64,... | collective-permute-start | bytes 393224 | tf_op jit(solution)/shard_map/ppermute | solution.py:25
  18.2 3.8 %collective-permute-start = (bf16[8,2,32,128]{3,2,1,0:T(8,128)(2,1)S(1)}, bf16[8,2,32,128]{3,2,1,0:T(8,128)(2,1)S(1)}, u32[]{:S(2)}, u32[]{:S(2)}) collective-permute-start(bf16[8,2,32,128]{3,2,1,0:T(8,128)(2,1)S(1)} %all-to-all-done.x0_ref), channel_id=1, source_target_pairs={{0,8},{8,16},{16,24},{24,32},{32,40},{40,48},{48,56},{56,64},{64,7... | collective-permute-start | bytes 393224 | tf_op jit(solution)/shard_map/ppermute | solution.py:25
  22.0 8.3 %collective-permute-done.1.x2_ref = bf16[8,2,32,128]{3,2,1,0:T(8,128)(2,1)S(1)} collective-permute-done((bf16[8,2,32,128]{3,2,1,0:T(8,128)(2,1)S(1)}, bf16[8,2,32,128]{3,2,1,0:T(8,128)(2,1)S(1)}, u32[]{:S(2)}, u32[]{:S(2)}) %collective-permute-start.1) | collective-permute-done | bytes 131104 | tf_op jit(solution)/shard_map/ppermute | solution.py:25
  30.3 3.3 %collective-permute-done.x1_ref = bf16[8,2,32,128]{3,2,1,0:T(8,128)(2,1)S(1)} collective-permute-done((bf16[8,2,32,128]{3,2,1,0:T(8,128)(2,1)S(1)}, bf16[8,2,32,128]{3,2,1,0:T(8,128)(2,1)S(1)}, u32[]{:S(2)}, u32[]{:S(2)}) %collective-permute-start) | collective-permute-done | bytes 131104 | tf_op jit(solution)/shard_map/ppermute | solution.py:25
  33.6 0.0 copy-start
  33.6 1.2 %copy-done = bf16[256,16,128]{2,1,0:T(8,128)(2,1)S(1)} copy-done((bf16[256,16,128]{2,1,0:T(8,128)(2,1)S(1)}, bf16[256,16,128]{2,1,0:T(8,128)(2,1)}, u32[]{:S(2)}) %copy-start) | copy-done | bytes 1048600
  34.8 0.0 copy-start.1
  34.8 1.2 %copy-done.1 = bf16[256,16,128]{2,1,0:T(8,128)(2,1)S(1)} copy-done((bf16[256,16,128]{2,1,0:T(8,128)(2,1)S(1)}, bf16[256,16,128]{2,1,0:T(8,128)(2,1)}, u32[]{:S(2)}) %copy-start.1) | copy-done | bytes 1048600
  36.0 13.8 %local_grads.1 = (bf16[4096,128]{1,0:T(8,128)(2,1)}, bf16[8,2,32,128]{3,2,1,0:T(8,128)(2,1)S(1)}, bf16[8,2,32,128]{3,2,1,0:T(8,128)(2,1)S(1)}, bf16[8,2,32,128]{3,2,1,0:T(8,128)(2,1)S(1)}) custom-call(s32[2]{0:T(128)S(1)} %fusion.1.prev_ref, bf16[4096,128]{1,0:T(8,128)(2,1)S(1)} %bitcast.3, bf16[4096,128]{1,0:T(8,128)(2,1)S(1)} %bitcast.4, ...), custom_call_target="tpu_custom_call" | custom-call | tf_op jit(solution)/shard_map/local_grads/pallas_call | solution.py:131
  49.8 2.9 %collective-permute-start.2 = (bf16[8,2,32,128]{3,2,1,0:T(8,128)(2,1)S(1)}, bf16[8,2,32,128]{3,2,1,0:T(8,128)(2,1)S(1)}, u32[]{:S(2)}, u32[]{:S(2)}) collective-permute-start(bf16[8,2,32,128]{3,2,1,0:T(8,128)(2,1)S(1)} %get-tuple-element.11), channel_id=1, source_target_pairs={{8,0},{16,8},{24,16},{32,24},{40,32},{48,40},{56,48},{64,56},{72,6... | collective-permute-start | bytes 393224 | tf_op jit(solution)/shard_map/ppermute | solution.py:25
  52.8 4.5 %collective-permute-start.3 = (bf16[8,2,32,128]{3,2,1,0:T(8,128)(2,1)S(1)}, bf16[8,2,32,128]{3,2,1,0:T(8,128)(2,1)S(1)}, u32[]{:S(2)}, u32[]{:S(2)}) collective-permute-start(bf16[8,2,32,128]{3,2,1,0:T(8,128)(2,1)S(1)} %get-tuple-element.12), channel_id=1, source_target_pairs={{16,0},{24,8},{32,16},{40,24},{48,32},{56,40},{64,48},{72,56},{80,... | collective-permute-start | bytes 393224 | tf_op jit(solution)/shard_map/ppermute | solution.py:25
  57.3 0.0 collective-permute-done.2
  57.3 5.2 %collective-permute-done.3 = bf16[8,2,32,128]{3,2,1,0:T(8,128)(2,1)S(1)} collective-permute-done((bf16[8,2,32,128]{3,2,1,0:T(8,128)(2,1)S(1)}, bf16[8,2,32,128]{3,2,1,0:T(8,128)(2,1)S(1)}, u32[]{:S(2)}, u32[]{:S(2)}) %collective-permute-start.3) | collective-permute-done | bytes 131104 | tf_op jit(solution)/shard_map/ppermute | solution.py:25
  62.5 0.1 add_convert_fusion
  62.6 9.2 %all_to_all.10.in_ref = bf16[8,2,32,128]{3,2,1,0:T(8,128)(2,1)} all-to-all(bf16[8,2,32,128]{3,2,1,0:T(8,128)(2,1)S(1)} %add_convert_fusion), channel_id=1, replica_groups=mesh['ctx'=64,'tp'=8] {'tp'}, dimensions={0} | all-to-all | bytes 262144 | tf_op jit(solution)/shard_map/all_to_all | solution.py:187
  71.8 1.7 %from_groups.1 = (bf16[32,8,128]{2,1,0:T(8,128)(2,1)}, bf16[32,8,128]{2,1,0:T(8,128)(2,1)}) custom-call(bf16[8,2,32,128]{3,2,1,0:T(8,128)(2,1)} %all_to_all.10.in_ref), custom_call_target="tpu_custom_call" | custom-call | tf_op jit(solution)/shard_map/from_groups/pallas_call | solution.py:188
  (2 shorter events, 0.0 us)
Async XLA Ops:
  2.4 10.6 %all-to-all-start = ((bf16[8,2,32,128]{3,2,1,0:T(8,128)(2,1)}), bf16[8,2,32,128]{3,2,1,0:T(8,128)(2,1)S(1)}, u32[]{:S(2)}, u32[]{:S(2)}) async-start(bf16[8,2,32,128]{3,2,1,0:T(8,128)(2,1)} %to_groups.1), calls=%async_computation | async-start | bytes 262144 | tf_op jit(solution)/shard_map/all_to_all | solution.py:168
  6.9 0.7 copy-start.2
  13.0 17.3 %collective-permute-start.1 = (bf16[8,2,32,128]{3,2,1,0:T(8,128)(2,1)S(1)}, bf16[8,2,32,128]{3,2,1,0:T(8,128)(2,1)S(1)}, u32[]{:S(2)}, u32[]{:S(2)}) collective-permute-start(bf16[8,2,32,128]{3,2,1,0:T(8,128)(2,1)S(1)} %all-to-all-done.x0_ref), channel_id=1, source_target_pairs={{0,16},{8,24},{16,32},{24,40},{32,48},{40,56},{48,64},{56,72},{64,... | collective-permute-start | bytes 393224 | tf_op jit(solution)/shard_map/ppermute | solution.py:25
  18.2 15.4 %collective-permute-start = (bf16[8,2,32,128]{3,2,1,0:T(8,128)(2,1)S(1)}, bf16[8,2,32,128]{3,2,1,0:T(8,128)(2,1)S(1)}, u32[]{:S(2)}, u32[]{:S(2)}) collective-permute-start(bf16[8,2,32,128]{3,2,1,0:T(8,128)(2,1)S(1)} %all-to-all-done.x0_ref), channel_id=1, source_target_pairs={{0,8},{8,16},{16,24},{24,32},{32,40},{40,48},{48,56},{56,64},{64,7... | collective-permute-start | bytes 393224 | tf_op jit(solution)/shard_map/ppermute | solution.py:25
  33.6 1.2 %copy-start = (bf16[256,16,128]{2,1,0:T(8,128)(2,1)S(1)}, bf16[256,16,128]{2,1,0:T(8,128)(2,1)}, u32[]{:S(2)}) copy-start(bf16[256,16,128]{2,1,0:T(8,128)(2,1)} %param.5) | copy-start | bytes 3145732
  34.8 1.2 %copy-start.1 = (bf16[256,16,128]{2,1,0:T(8,128)(2,1)S(1)}, bf16[256,16,128]{2,1,0:T(8,128)(2,1)}, u32[]{:S(2)}) copy-start(bf16[256,16,128]{2,1,0:T(8,128)(2,1)} %param.8) | copy-start | bytes 3145732
  49.8 7.5 %collective-permute-start.2 = (bf16[8,2,32,128]{3,2,1,0:T(8,128)(2,1)S(1)}, bf16[8,2,32,128]{3,2,1,0:T(8,128)(2,1)S(1)}, u32[]{:S(2)}, u32[]{:S(2)}) collective-permute-start(bf16[8,2,32,128]{3,2,1,0:T(8,128)(2,1)S(1)} %get-tuple-element.11), channel_id=1, source_target_pairs={{8,0},{16,8},{24,16},{32,24},{40,32},{48,40},{56,48},{64,56},{72,6... | collective-permute-start | bytes 393224 | tf_op jit(solution)/shard_map/ppermute | solution.py:25
  52.8 9.8 %collective-permute-start.3 = (bf16[8,2,32,128]{3,2,1,0:T(8,128)(2,1)S(1)}, bf16[8,2,32,128]{3,2,1,0:T(8,128)(2,1)S(1)}, u32[]{:S(2)}, u32[]{:S(2)}) collective-permute-start(bf16[8,2,32,128]{3,2,1,0:T(8,128)(2,1)S(1)} %get-tuple-element.12), channel_id=1, source_target_pairs={{16,0},{24,8},{32,16},{40,24},{48,32},{56,40},{64,48},{72,56},{80,... | collective-permute-start | bytes 393224 | tf_op jit(solution)/shard_map/ppermute | solution.py:25

commit v2 on v1

v2 whole, which is shorter than its diff:
```python
import functools
import math

import jax
import jax.numpy as jnp
from jax import lax
from jax.experimental import pallas as pl
from jax.experimental.pallas import tpu as pltpu
from jax.sharding import PartitionSpec as P

BLK = 128
BLK_DEV = 2
BACK = 4
LOG2E = math.log2(math.e)
LOW = -3.0e38
OFF = 1.0e30

VMEM = pl.BlockSpec(memory_space=pltpu.VMEM)
SMEM = pl.BlockSpec(memory_space=pltpu.SMEM)
HBM = pl.BlockSpec(memory_space=pltpu.HBM)


def passed_along(block, axis, distance):
    devices = range(lax.axis_size(axis))
    route = [(i - distance, i) for i in devices if i - distance in devices]
    return lax.ppermute(block, axis, route)


def to_groups(k_ref, v_ref, out_ref, wide):
    for which, ref in enumerate((k_ref, v_ref)):
        wide[...] = ref[...].astype(jnp.float32)
        for g in range(wide.shape[1]):
            out_ref[g, which] = wide[:, g, :].astype(out_ref.dtype)


def from_groups(in_ref, k_ref, v_ref, wide):
    for which, ref in enumerate((k_ref, v_ref)):
        for g in range(wide.shape[1]):
            wide[:, g, :] = in_ref[g, which].astype(jnp.float32)
        ref[...] = wide[...].astype(ref.dtype)


def stage(q_hbm, g_hbm, q_ref, g_ref, sem):
    copies = [
        pltpu.make_async_copy(src, dst, sem.at[i])
        for i, (src, dst) in enumerate(((q_hbm, q_ref), (g_hbm, g_ref)))
    ]
    for copy in copies:
        copy.start()
    for copy in copies:
        copy.wait()


NT = (((1,), (1,)), ((), ()))
SPAN = (BACK + 1) * BLK
LOCAL = BLK_DEV * BLK
SPANS = [slice(o * BLK, (o + 1) * BLK) for o in range(BACK + 1)]


def scores_kernel(prev_ref, q_ref, g_ref, x0_ref, x1_ref, x2_ref,
                  y1_ref, y2_ref, d_ref, own_ref,
                  kk, vv, dk, dv, st_buf, dp_buf, p_buf, *, heads, rows):
    total_rows, head_size = q_ref.shape
    scale = 1.0 / math.sqrt(head_size)
    factor = scale * LOG2E
    f32 = jnp.float32
    low = kk.dtype
    chunks = total_rows // rows
    per_block = chunks // BLK_DEV
    far = BLK_DEV * LOCAL

    for i, ref in enumerate((x2_ref, x1_ref, x0_ref)):
        kk[i * LOCAL:(i + 1) * LOCAL] = ref[:, 0].reshape(LOCAL, head_size)
        vv[i * LOCAL:(i + 1) * LOCAL] = ref[:, 1].reshape(LOCAL, head_size)
    dk[...] = jnp.zeros_like(dk)
    dv[...] = jnp.zeros_like(dv)
    off = [
        [jnp.where(prev_ref[b] >= BACK - o, 0.0, OFF).astype(f32) for o in range(BACK)] + [None]
        for b in range(BLK_DEV)
    ]

    def place(c):
        base = c // per_block * BLK
        return slice(base, base + SPAN), slice(c * rows, (c + 1) * rows)

    def score_part(c):
        window, here = place(c)
        st_buf[c % 2] = lax.dot_general(kk[window], q_ref[here], NT, preferred_element_type=f32)

    def dprob_part(c):
        window, here = place(c)
        dp_buf[c % 2] = lax.dot_general(vv[window], g_ref[here], NT, preferred_element_type=f32)

    def exp_part(c):
        st = st_buf.at[c % 2]
        shut = off[c // per_block]
        key = lax.broadcasted_iota(jnp.int32, (BLK, rows), 0) * heads
        row = lax.broadcasted_iota(jnp.int32, (BLK, rows), 1) + c % per_block * rows
        own = jnp.where(key <= row, st[SPANS[BACK]], -OFF)
        top = jnp.max(own, axis=0, keepdims=True)
        for o in range(BACK):
            top = jnp.maximum(top, jnp.max(st[SPANS[o]], axis=0, keepdims=True) - shut[o])
        shift = top * factor
        total = jnp.zeros((1, rows), f32)
        for o in range(BACK + 1):
            if o == BACK:
                e = jnp.exp2(own * factor - shift)
            else:
                e = jnp.exp2(st[SPANS[o]] * factor - (shift + shut[o]))
            total = total + jnp.sum(e, axis=0, keepdims=True)
            st[SPANS[o]] = e
        return 1.0 / total

    def near(c):
        return BACK - c // per_block

    def prob_part(c, inv):
        st, dp = st_buf.at[c % 2], dp_buf.at[c % 2]
        delta = jnp.zeros((1, rows), f32)
        for o in range(BACK + 1):
            p_low = (st[SPANS[o]] * inv).astype(low)
            if o < near(c):
                p_buf[c % 2, SPANS[o]] = p_low
            else:
                own_ref[c, SPANS[o - BACK + 1]] = p_low
            delta = delta + jnp.sum(p_low.astype(f32) * dp[SPANS[o]], axis=0, keepdims=True)
        return delta

    def dscore_part(c, inv, delta):
        st, dp = st_buf.at[c % 2], dp_buf.at[c % 2]
        for o in range(BACK + 1):
            ds = st[SPANS[o]] * inv * (dp[SPANS[o]] - delta) * scale
            d_ref[c, SPANS[o]] = ds.astype(low)

    def value_part(c):
        window, here = place(c)
        count = near(c) * BLK
        dv[window.start:far] += jnp.dot(p_buf[c % 2, :count], g_ref[here], preferred_element_type=f32)

    def key_part(c):
        window, here = place(c)
        count = near(c) * BLK
        dk[window.start:far] += jnp.dot(d_ref[c, :count], q_ref[here], preferred_element_type=f32)

    for c in range(-1, chunks + 1):
        first, inside, last = c + 1 < chunks, 0 <= c < chunks, c >= 1
        if first:
            score_part(c + 1)
        if inside:
            inv = exp_part(c)
        if last:
            value_part(c - 1)
        if first:
            dprob_part(c + 1)
        if inside:
            delta = prob_part(c, inv)
        if last:
            key_part(c - 1)
        if inside:
            dscore_part(c, inv, delta)
    for i, ref in enumerate((y2_ref, y1_ref)):
        k = dk[i * LOCAL:(i + 1) * LOCAL]
        v = dv[i * LOCAL:(i + 1) * LOCAL]
        ref[:, 0] = k.astype(low).reshape(ref.shape[0], -1, head_size)
        ref[:, 1] = v.astype(low).reshape(ref.shape[0], -1, head_size)


def finish_kernel(q_ref, g_ref, x0_ref, x1_ref, x2_ref, d_ref, own_ref,
                  dq_hbm, y0_ref, dq_all, kt, dk, dv, sem, *, rows, pieces):
    total_rows, head_size = q_ref.shape
    f32 = jnp.float32
    low = kt.dtype
    chunks = total_rows // rows
    per_block = chunks // BLK_DEV
    piece = total_rows // pieces
    per_piece = chunks // pieces

    def put(i):
        part = pl.ds(i * piece, piece)
        return pltpu.make_async_copy(dq_all.at[part], dq_hbm.at[part], sem.at[i])

    for i, ref in enumerate((x2_ref, x1_ref, x0_ref)):
        k = ref[:, 0].reshape(LOCAL, head_size)
        kt[:, i * LOCAL:(i + 1) * LOCAL] = k.astype(f32).T.astype(low)
    dk[...] = jnp.zeros_like(dk)
    dv[...] = jnp.zeros_like(dv)
    for c in range(chunks):
        block = c // per_block
        here = slice(c * rows, (c + 1) * rows)
        held = slice(0, (block + 1) * BLK)
        d_low = d_ref[c]
        dqt = jnp.dot(kt[:, block * BLK:block * BLK + SPAN], d_low, preferred_element_type=f32)
        dk[held] += jnp.dot(d_low[SPAN - held.stop:], q_ref[here], preferred_element_type=f32)
        dv[held] += jnp.dot(own_ref[c, LOCAL - held.stop:], g_ref[here], preferred_element_type=f32)
        dq_all[here] = dqt.T.astype(low)
        if (c + 1) % per_piece == 0:
            put(c // per_piece).start()
    y0_ref[:, 0] = dk[...].astype(low).reshape(y0_ref.shape[0], -1, head_size)
    y0_ref[:, 1] = dv[...].astype(low).reshape(y0_ref.shape[0], -1, head_size)
    for i in range(pieces):
        put(i).wait()


def staged(q, g):
    return pl.pallas_call(
        stage,
        out_shape=(jax.ShapeDtypeStruct(q.shape, q.dtype), jax.ShapeDtypeStruct(g.shape, g.dtype)),
        in_specs=[HBM, HBM],
        out_specs=(VMEM, VMEM),
        scratch_shapes=[pltpu.SemaphoreType.DMA((2,))],
        cost_estimate=pl.CostEstimate(flops=0, bytes_accessed=4 * q.size * 2, transcendentals=0),
        compiler_params=pltpu.CompilerParams(vmem_limit_bytes=8 << 20),
        name="stage",
    )(q, g)


def remote_grads(prev, q, g, x0, x1, x2, heads, rows):
    head_size = q.shape[1]
    keys = 3 * LOCAL
    chunks = q.shape[0] // rows
    low = q.dtype
    f32 = jnp.float32
    pairs = 2 * BACK + 2
    return pl.pallas_call(
        functools.partial(scores_kernel, heads=heads, rows=rows),
        out_shape=(
            jax.ShapeDtypeStruct(x0.shape, low),
            jax.ShapeDtypeStruct(x0.shape, low),
            jax.ShapeDtypeStruct((chunks, SPAN, rows), low),
            jax.ShapeDtypeStruct((chunks, LOCAL, rows), low),
        ),
        in_specs=[SMEM] + [VMEM] * 5,
        out_specs=(VMEM,) * 4,
        scratch_shapes=[
            pltpu.VMEM((keys, head_size), low),
            pltpu.VMEM((keys, head_size), low),
            pltpu.VMEM((2 * LOCAL, head_size), f32),
            pltpu.VMEM((2 * LOCAL, head_size), f32),
            pltpu.VMEM((2, SPAN, rows), f32),
            pltpu.VMEM((2, SPAN, rows), f32),
            pltpu.VMEM((2, BACK * BLK, rows), low),
        ],
        cost_estimate=pl.CostEstimate(
            flops=2 * 4 * SPAN * q.size, bytes_accessed=8 * q.size, transcendentals=SPAN * q.shape[0]
        ),
        compiler_params=pltpu.CompilerParams(vmem_limit_bytes=24 << 20),
        name="remote_grads",
    )(prev, q, g, x0, x1, x2)


def own_grads(q, g, x0, x1, x2, d_low, own, pieces=4):
    head_size = q.shape[1]
    rows = d_low.shape[2]
    low = q.dtype
    f32 = jnp.float32
    return pl.pallas_call(
        functools.partial(finish_kernel, rows=rows, pieces=pieces),
        out_shape=(jax.ShapeDtypeStruct(q.shape, low), jax.ShapeDtypeStruct(x0.shape, low)),
        in_specs=[VMEM] * 7,
        out_specs=(HBM, VMEM),
        scratch_shapes=[
            pltpu.VMEM(q.shape, low),
            pltpu.VMEM((head_size, 3 * LOCAL), low),
            pltpu.VMEM((LOCAL, head_size), f32),
            pltpu.VMEM((LOCAL, head_size), f32),
            pltpu.SemaphoreType.DMA((pieces,)),
        ],
        cost_estimate=pl.CostEstimate(
            flops=2 * 2 * SPAN * q.size, bytes_accessed=8 * q.size, transcendentals=0
        ),
        compiler_params=pltpu.CompilerParams(vmem_limit_bytes=16 << 20),
        name="own_grads",
    )(q, g, x0, x1, x2, d_low, own)


def local_grads(prev, q, g, x0, x1, x2, heads, rows=512):
    y1, y2, d_low, own = remote_grads(prev, q, g, x0, x1, x2, heads, rows)
    dq, y0 = own_grads(q, g, x0, x1, x2, d_low, own)
    return dq, y0, y1, y2


def on_device(queries, keys, values, output_gradient, doc_blocks):
    tok_count, heads, head_size = queries.shape
    tok_part, groups, _ = keys.shape
    low = queries.dtype
    packed = pl.pallas_call(
        to_groups,
        out_shape=jax.ShapeDtypeStruct((groups, 2, tok_part, head_size), low),
        in_specs=[VMEM, VMEM],
        out_specs=VMEM,
        scratch_shapes=[pltpu.VMEM(keys.shape, jnp.float32)],
        name="to_groups",
    )(keys, values)
    x0 = lax.all_to_all(packed, "tp", split_axis=0, concat_axis=0, tiled=True)
    x1 = passed_along(x0, "ctx", 1)
    x2 = passed_along(x0, "ctx", 2)
    docs = doc_blocks.shape[0]
    upto = jnp.arange(docs)[:, None] >= jnp.arange(docs)[None, :]
    ends = jnp.sum(jnp.where(upto, doc_blocks[None, :], 0), axis=1)
    mine = lax.axis_index("ctx") * BLK_DEV + jnp.arange(BLK_DEV, dtype=jnp.int32)
    start = jnp.max(jnp.where(ends[None, :] <= mine[:, None], ends[None, :], 0), axis=1)
    prev = (mine - start).astype(jnp.int32)
    q, g = staged(
        queries.reshape(tok_count * heads, head_size),
        output_gradient.reshape(tok_count * heads, head_size),
    )
    y1, y2, d_low, own = remote_grads(prev, q, g, x0, x1, x2, heads, 256)
    r2 = passed_along(y2, "ctx", -2)
    r1 = passed_along(y1, "ctx", -1)
    dq, y0 = own_grads(q, g, x0, x1, x2, d_low, own)
    f32 = jnp.float32
    summed = (y0.astype(f32) + r1.astype(f32) + r2.astype(f32)).astype(low)
    back = lax.all_to_all(summed, "tp", split_axis=0, concat_axis=0, tiled=True)
    key_gradient, value_gradient = pl.pallas_call(
        from_groups,
        out_shape=(
            jax.ShapeDtypeStruct(keys.shape, low),
            jax.ShapeDtypeStruct(values.shape, low),
        ),
        in_specs=[VMEM],
        out_specs=(VMEM, VMEM),
        scratch_shapes=[pltpu.VMEM(keys.shape, jnp.float32)],
        name="from_groups",
    )(back)
    return dq.reshape(queries.shape), key_gradient, value_gradient


def solution(mesh):
    return jax.shard_map(
        on_device,
        mesh=mesh,
        in_specs=(
            P("ctx", "tp", None),
            P(("ctx", "tp"), None, None),
            P(("ctx", "tp"), None, None),
            P("ctx", "tp", None),
            P(),
        ),
        out_specs=(
            P("ctx", "tp", None),
            P(("ctx", "tp"), None, None),
            P(("ctx", "tp"), None, None),
        ),
        check_vma=False,
    )
```

time: 73.9 us -> 65.9 us (0.89)
  waiting for transfers between devices: 21.9 us -> 16.8 us
  Pallas kernels: 17.3 us -> 14.3 us
    pallas_call x1 -> x3, Pallas kernels: 13.8 us -> 10.8 us  [the longest x1 8.13 us: remote_grads(): pl.pallas_call(functools.partial(scores_kernel, heads=heads, rows=rows),...]
    all_to_all x1, waiting for transfers between devices: 5.14 us -> 2.51 us  [on_device(): x0 = lax.all_to_all(packed, 'tp', split_axis=0, concat_axis=0, tiled=True)]
    ppermute x4, waiting for transfers between devices: 16.8 us -> 14.3 us  [passed_along(): return lax.ppermute(block, axis, route)]
    unnamed x6 -> x4, local copies, waits for them, and re-layouts: 3.1 us -> 2.44 us
  transfers between devices with their start and end apart: 5 -> 5, of which waited for: 4 -> 4; matrix products, arithmetic and copies ran while one was open for 0% -> 1% of each run, Pallas kernels for 0% -> 4%
where the time goes in v2:
time: 65.9 us; the launch traced here: 65.4 us
  starting transfers between devices  21 us (32%)
  waiting for transfers between devices  16.8 us (25%)
  Pallas kernels  14.3 us (22%)
  blocking collectives  9.17 us (14%)
  local copies, waits for them, and re-layouts  2.44 us (4%)
  other arithmetic  1.01 us (2%)
  between operations  0.73 us (1%)
    ppermute x4, starting transfers between devices, passed_along(): return lax.ppermute(block, axis, route)  16.5 us
    ppermute x4, waiting for transfers between devices, passed_along(): return lax.ppermute(block, axis, route)  14.3 us
    all_to_all x1, blocking collectives, on_device(): back = lax.all_to_all(summed, 'tp', split_axis=0, concat_axis=0, tiled=True)  9.17 us
    pallas_call x1, Pallas kernels, remote_grads(): pl.pallas_call(functools.partial(scores_kernel, heads=heads, rows=rows),...  8.13 us
    all_to_all x1, starting transfers between devices, on_device(): x0 = lax.all_to_all(packed, 'tp', split_axis=0, concat_axis=0, tiled=True)  4.47 us
    pallas_call x1, Pallas kernels, own_grads(): pl.pallas_call(functools.partial(finish_kernel, rows=rows, pieces=pieces)...  2.54 us
    all_to_all x1, waiting for transfers between devices, on_device(): x0 = lax.all_to_all(packed, 'tp', split_axis=0, concat_axis=0, tiled=True)  2.51 us
    unnamed x4, local copies, waits for them, and re-layouts  2.44 us
  transfers between devices with their start and end apart: 5, of which 4 were waited for; matrix products, arithmetic and copies ran while one was open for 1% of the time, Pallas kernels for 4%

profile of v2, /device:TPU:6, one launch (start us, length us, event | category | flops | bytes accessed | tf_op | source)
XLA Modules:
  0.0 65.4 jit_solution(10527627357529570699)
XLA Ops:
  0.6 1.8 %to_groups.1 = bf16[8,2,32,128]{3,2,1,0:T(8,128)(2,1)} custom-call(bf16[32,8,128]{2,1,0:T(8,128)(2,1)} %k_ref.1, bf16[32,8,128]{2,1,0:T(8,128)(2,1)} %v_ref.1), custom_call_target="tpu_custom_call" | custom-call | tf_op jit(solution)/shard_map/to_groups/pallas_call | solution.py:286
  2.4 4.5 %all-to-all-start = ((bf16[8,2,32,128]{3,2,1,0:T(8,128)(2,1)}), bf16[8,2,32,128]{3,2,1,0:T(8,128)(2,1)S(1)}, u32[]{:S(2)}, u32[]{:S(2)}) async-start(bf16[8,2,32,128]{3,2,1,0:T(8,128)(2,1)} %to_groups.1), calls=%async_computation | async-start | bytes 262144 | tf_op jit(solution)/shard_map/all_to_all | solution.py:294
  6.9 0.8 %select_reduce_fusion = s32[64]{0:T(128)S(1)} fusion(s32[64]{0:T(128)} %param.9), kind=kLoop, calls=%fused_computation.1 | loop fusion | flops 12224 | bytes 512 | tf_op jit(solution)/shard_map/reduce_sum | solution.py:299
  7.7 0.0 copy-start
  7.7 1.2 %copy-done = bf16[256,16,128]{2,1,0:T(8,128)(2,1)S(1)} copy-done((bf16[256,16,128]{2,1,0:T(8,128)(2,1)S(1)}, bf16[256,16,128]{2,1,0:T(8,128)(2,1)}, u32[]{:S(2)}) %copy-start) | copy-done | bytes 1048600
  8.9 0.0 copy-start.1
  8.9 1.2 %copy-done.1 = bf16[256,16,128]{2,1,0:T(8,128)(2,1)S(1)} copy-done((bf16[256,16,128]{2,1,0:T(8,128)(2,1)S(1)}, bf16[256,16,128]{2,1,0:T(8,128)(2,1)}, u32[]{:S(2)}) %copy-start.1) | copy-done | bytes 1048600
  10.1 0.2 stage.1
  10.3 0.2 fusion
  10.5 2.5 %all-to-all-done.x0_ref = bf16[8,2,32,128]{3,2,1,0:T(8,128)(2,1)S(1)} async-done(((bf16[8,2,32,128]{3,2,1,0:T(8,128)(2,1)}), bf16[8,2,32,128]{3,2,1,0:T(8,128)(2,1)S(1)}, u32[]{:S(2)}, u32[]{:S(2)}) %all-to-all-start) | async-done | bytes 131104 | tf_op jit(solution)/shard_map/all_to_all | solution.py:294
  13.0 5.2 %collective-permute-start.1 = (bf16[8,2,32,128]{3,2,1,0:T(8,128)(2,1)S(1)}, bf16[8,2,32,128]{3,2,1,0:T(8,128)(2,1)S(1)}, u32[]{:S(2)}, u32[]{:S(2)}) collective-permute-start(bf16[8,2,32,128]{3,2,1,0:T(8,128)(2,1)S(1)} %all-to-all-done.x0_ref), channel_id=1, source_target_pairs={{0,16},{8,24},{16,32},{24,40},{32,48},{40,56},{48,64},{56,72},{64,... | collective-permute-start | bytes 393224 | tf_op jit(solution)/shard_map/ppermute | solution.py:26
  18.2 3.8 %collective-permute-start = (bf16[8,2,32,128]{3,2,1,0:T(8,128)(2,1)S(1)}, bf16[8,2,32,128]{3,2,1,0:T(8,128)(2,1)S(1)}, u32[]{:S(2)}, u32[]{:S(2)}) collective-permute-start(bf16[8,2,32,128]{3,2,1,0:T(8,128)(2,1)S(1)} %all-to-all-done.x0_ref), channel_id=1, source_target_pairs={{0,8},{8,16},{16,24},{24,32},{32,40},{40,48},{48,56},{56,64},{64,7... | collective-permute-start | bytes 393224 | tf_op jit(solution)/shard_map/ppermute | solution.py:26
  22.0 8.3 %collective-permute-done.1.x2_ref = bf16[8,2,32,128]{3,2,1,0:T(8,128)(2,1)S(1)} collective-permute-done((bf16[8,2,32,128]{3,2,1,0:T(8,128)(2,1)S(1)}, bf16[8,2,32,128]{3,2,1,0:T(8,128)(2,1)S(1)}, u32[]{:S(2)}, u32[]{:S(2)}) %collective-permute-start.1) | collective-permute-done | bytes 131104 | tf_op jit(solution)/shard_map/ppermute | solution.py:26
  30.3 3.3 %collective-permute-done.x1_ref = bf16[8,2,32,128]{3,2,1,0:T(8,128)(2,1)S(1)} collective-permute-done((bf16[8,2,32,128]{3,2,1,0:T(8,128)(2,1)S(1)}, bf16[8,2,32,128]{3,2,1,0:T(8,128)(2,1)S(1)}, u32[]{:S(2)}, u32[]{:S(2)}) %collective-permute-start) | collective-permute-done | bytes 131104 | tf_op jit(solution)/shard_map/ppermute | solution.py:26
  33.6 8.1 %remote_grads.1 = (bf16[8,2,32,128]{3,2,1,0:T(8,128)(2,1)S(1)}, bf16[8,2,32,128]{3,2,1,0:T(8,128)(2,1)S(1)}, bf16[16,640,256]{2,1,0:T(8,128)(2,1)S(1)}, bf16[16,256,256]{2,1,0:T(8,128)(2,1)S(1)}) custom-call(s32[2]{0:T(128)S(1)} %fusion.1.prev_ref, bf16[4096,128]{1,0:T(8,128)(2,1)S(1)} %get-tuple-element.13.q_ref, ...), custom_call_target="tpu_custom_call" | custom-call | flops 2684354560 | bytes 4194304 | tf_op jit(solution)/shard_map/remote_grads/pallas_call | solution.py:224
  41.7 2.9 %collective-permute-start.2 = (bf16[8,2,32,128]{3,2,1,0:T(8,128)(2,1)S(1)}, bf16[8,2,32,128]{3,2,1,0:T(8,128)(2,1)S(1)}, u32[]{:S(2)}, u32[]{:S(2)}) collective-permute-start(bf16[8,2,32,128]{3,2,1,0:T(8,128)(2,1)S(1)} %get-tuple-element.19), channel_id=1, source_target_pairs={{8,0},{16,8},{24,16},{32,24},{40,32},{48,40},{56,48},{64,56},{72,6... | collective-permute-start | bytes 393224 | tf_op jit(solution)/shard_map/ppermute | solution.py:26
  44.7 4.5 %collective-permute-start.3 = (bf16[8,2,32,128]{3,2,1,0:T(8,128)(2,1)S(1)}, bf16[8,2,32,128]{3,2,1,0:T(8,128)(2,1)S(1)}, u32[]{:S(2)}, u32[]{:S(2)}) collective-permute-start(bf16[8,2,32,128]{3,2,1,0:T(8,128)(2,1)S(1)} %get-tuple-element.20), channel_id=1, source_target_pairs={{16,0},{24,8},{32,16},{40,24},{48,32},{56,40},{64,48},{72,56},{80,... | collective-permute-start | bytes 393224 | tf_op jit(solution)/shard_map/ppermute | solution.py:26
  49.2 2.5 %own_grads.1 = (bf16[4096,128]{1,0:T(8,128)(2,1)}, bf16[8,2,32,128]{3,2,1,0:T(8,128)(2,1)S(1)}) custom-call(bf16[4096,128]{1,0:T(8,128)(2,1)S(1)} %get-tuple-element.13.q_ref, bf16[4096,128]{1,0:T(8,128)(2,1)S(1)} %get-tuple-element.14.g_ref, bf16[8,2,32,128]{3,2,1,0:T(8,128)(2,1)S(1)} %all-to-all-done.x0_ref, ...), custom_call_target="tpu_custom_call" | custom-call | flops 1342177280 | bytes 4194304 | tf_op jit(solution)/shard_map/own_grads/pallas_call | solution.py:256
  51.8 0.0 collective-permute-done.2
  51.8 2.7 %collective-permute-done.3 = bf16[8,2,32,128]{3,2,1,0:T(8,128)(2,1)S(1)} collective-permute-done((bf16[8,2,32,128]{3,2,1,0:T(8,128)(2,1)S(1)}, bf16[8,2,32,128]{3,2,1,0:T(8,128)(2,1)S(1)}, u32[]{:S(2)}, u32[]{:S(2)}) %collective-permute-start.3) | collective-permute-done | bytes 131104 | tf_op jit(solution)/shard_map/ppermute | solution.py:26
  54.5 0.1 add_convert_fusion
  54.6 9.2 %all_to_all.10.in_ref = bf16[8,2,32,128]{3,2,1,0:T(8,128)(2,1)} all-to-all(bf16[8,2,32,128]{3,2,1,0:T(8,128)(2,1)S(1)} %add_convert_fusion), channel_id=1, replica_groups=mesh['ctx'=64,'tp'=8] {'tp'}, dimensions={0} | all-to-all | bytes 262144 | tf_op jit(solution)/shard_map/all_to_all | solution.py:313
  63.7 1.7 %from_groups.1 = (bf16[32,8,128]{2,1,0:T(8,128)(2,1)}, bf16[32,8,128]{2,1,0:T(8,128)(2,1)}) custom-call(bf16[8,2,32,128]{3,2,1,0:T(8,128)(2,1)} %all_to_all.10.in_ref), custom_call_target="tpu_custom_call" | custom-call | tf_op jit(solution)/shard_map/from_groups/pallas_call | solution.py:314
  (2 shorter events, 0.0 us)
Async XLA Ops:
  2.4 10.6 %all-to-all-start = ((bf16[8,2,32,128]{3,2,1,0:T(8,128)(2,1)}), bf16[8,2,32,128]{3,2,1,0:T(8,128)(2,1)S(1)}, u32[]{:S(2)}, u32[]{:S(2)}) async-start(bf16[8,2,32,128]{3,2,1,0:T(8,128)(2,1)} %to_groups.1), calls=%async_computation | async-start | bytes 262144 | tf_op jit(solution)/shard_map/all_to_all | solution.py:294
  7.7 1.2 %copy-start = (bf16[256,16,128]{2,1,0:T(8,128)(2,1)S(1)}, bf16[256,16,128]{2,1,0:T(8,128)(2,1)}, u32[]{:S(2)}) copy-start(bf16[256,16,128]{2,1,0:T(8,128)(2,1)} %param.5) | copy-start | bytes 3145732
  8.9 1.2 %copy-start.1 = (bf16[256,16,128]{2,1,0:T(8,128)(2,1)S(1)}, bf16[256,16,128]{2,1,0:T(8,128)(2,1)}, u32[]{:S(2)}) copy-start(bf16[256,16,128]{2,1,0:T(8,128)(2,1)} %param.8) | copy-start | bytes 3145732
  13.0 17.3 %collective-permute-start.1 = (bf16[8,2,32,128]{3,2,1,0:T(8,128)(2,1)S(1)}, bf16[8,2,32,128]{3,2,1,0:T(8,128)(2,1)S(1)}, u32[]{:S(2)}, u32[]{:S(2)}) collective-permute-start(bf16[8,2,32,128]{3,2,1,0:T(8,128)(2,1)S(1)} %all-to-all-done.x0_ref), channel_id=1, source_target_pairs={{0,16},{8,24},{16,32},{24,40},{32,48},{40,56},{48,64},{56,72},{64,... | collective-permute-start | bytes 393224 | tf_op jit(solution)/shard_map/ppermute | solution.py:26
  18.2 15.4 %collective-permute-start = (bf16[8,2,32,128]{3,2,1,0:T(8,128)(2,1)S(1)}, bf16[8,2,32,128]{3,2,1,0:T(8,128)(2,1)S(1)}, u32[]{:S(2)}, u32[]{:S(2)}) collective-permute-start(bf16[8,2,32,128]{3,2,1,0:T(8,128)(2,1)S(1)} %all-to-all-done.x0_ref), channel_id=1, source_target_pairs={{0,8},{8,16},{16,24},{24,32},{32,40},{40,48},{48,56},{56,64},{64,7... | collective-permute-start | bytes 393224 | tf_op jit(solution)/shard_map/ppermute | solution.py:26
  41.7 10.1 %collective-permute-start.2 = (bf16[8,2,32,128]{3,2,1,0:T(8,128)(2,1)S(1)}, bf16[8,2,32,128]{3,2,1,0:T(8,128)(2,1)S(1)}, u32[]{:S(2)}, u32[]{:S(2)}) collective-permute-start(bf16[8,2,32,128]{3,2,1,0:T(8,128)(2,1)S(1)} %get-tuple-element.19), channel_id=1, source_target_pairs={{8,0},{16,8},{24,16},{32,24},{40,32},{48,40},{56,48},{64,56},{72,6... | collective-permute-start | bytes 393224 | tf_op jit(solution)/shard_map/ppermute | solution.py:26
  44.7 9.8 %collective-permute-start.3 = (bf16[8,2,32,128]{3,2,1,0:T(8,128)(2,1)S(1)}, bf16[8,2,32,128]{3,2,1,0:T(8,128)(2,1)S(1)}, u32[]{:S(2)}, u32[]{:S(2)}) collective-permute-start(bf16[8,2,32,128]{3,2,1,0:T(8,128)(2,1)S(1)} %get-tuple-element.20), channel_id=1, source_target_pairs={{16,0},{24,8},{32,16},{40,24},{48,32},{56,40},{64,48},{72,56},{80,... | collective-permute-start | bytes 393224 | tf_op jit(solution)/shard_map/ppermute | solution.py:26

commit v3 on v2

--- a/solution.py
+++ b/solution.py
@@ -12,7 +12,6 @@
 BLK_DEV = 2
 BACK = 4
 LOG2E = math.log2(math.e)
-LOW = -3.0e38
 OFF = 1.0e30
 
 VMEM = pl.BlockSpec(memory_space=pltpu.VMEM)
@@ -57,21 +56,62 @@
 SPANS = [slice(o * BLK, (o + 1) * BLK) for o in range(BACK + 1)]
 
 
-def scores_kernel(prev_ref, q_ref, g_ref, x0_ref, x1_ref, x2_ref,
+def block_scores(st, factor):
+    top = jnp.max(st, axis=0, keepdims=True) * factor
+    e = jnp.exp2(st * factor - top)
+    return e, top, jnp.sum(e, axis=0, keepdims=True)
+
+
+def part_kernel(q_ref, g_ref, x_ref, e_ref, dp_ref, top_ref, sum_ref, st_buf, *, heads, rows, own):
+    total_rows, head_size = q_ref.shape
+    factor = LOG2E / math.sqrt(head_size)
+    f32 = jnp.float32
+    chunks = total_rows // rows
+    per_block = chunks // BLK_DEV
+    k = x_ref[:, 0].reshape(LOCAL, head_size)
+    v = x_ref[:, 1].reshape(LOCAL, head_size)
+
+    def count(c):
+        return c // per_block + 1 if own else BLK_DEV
+
+    def products(c):
+        here, size = slice(c * rows, (c + 1) * rows), count(c) * BLK
+        st_buf[c % 2, :size] = lax.dot_general(k[:size], q_ref[here], NT, preferred_element_type=f32)
+        dp_ref[c, :size] = lax.dot_general(v[:size], g_ref[here], NT, preferred_element_type=f32)
+
+    def exponentials(c):
+        for j in range(count(c)):
+            st = st_buf[c % 2, SPANS[j]]
+            if own and j == c // per_block:
+                key = lax.broadcasted_iota(jnp.int32, (BLK, rows), 0) * heads
+                row = lax.broadcasted_iota(jnp.int32, (BLK, rows), 1) + c % per_block * rows
+                st = jnp.where(key <= row, st, -OFF)
+            e, top, total = block_scores(st, factor)
+            e_ref[c, SPANS[j]] = e
+            top_ref[c, j:j + 1] = top
+            sum_ref[c, j:j + 1] = total
+
+    products(0)
+    for c in range(chunks):
+        if c + 1 < chunks:
+            products(c + 1)
+        exponentials(c)
+
+
+def scores_kernel(prev_ref, q_ref, g_ref, x2_ref, e0_ref, dp0_ref, top0_ref, sum0_ref,
+                  e1_ref, dp1_ref, top1_ref, sum1_ref,
                   y1_ref, y2_ref, d_ref, own_ref,
-                  kk, vv, dk, dv, st_buf, dp_buf, p_buf, *, heads, rows):
+                  dk, dv, st_buf, e_buf, dp_buf, p_buf, *, heads, rows):
     total_rows, head_size = q_ref.shape
     scale = 1.0 / math.sqrt(head_size)
     factor = scale * LOG2E
     f32 = jnp.float32
-    low = kk.dtype
+    low = q_ref.dtype
     chunks = total_rows // rows
     per_block = chunks // BLK_DEV
     far = BLK_DEV * LOCAL
-
-    for i, ref in enumerate((x2_ref, x1_ref, x0_ref)):
-        kk[i * LOCAL:(i + 1) * LOCAL] = ref[:, 0].reshape(LOCAL, head_size)
-        vv[i * LOCAL:(i + 1) * LOCAL] = ref[:, 1].reshape(LOCAL, head_size)
+    k = x2_ref[:, 0].reshape(LOCAL, head_size)
+    v = x2_ref[:, 1].reshape(LOCAL, head_size)
     dk[...] = jnp.zeros_like(dk)
     dv[...] = jnp.zeros_like(dv)
     off = [
@@ -79,90 +119,91 @@
         for b in range(BLK_DEV)
     ]
 
-    def place(c):
-        base = c // per_block * BLK
-        return slice(base, base + SPAN), slice(c * rows, (c + 1) * rows)
+    def away(c):
+        return BACK - c // per_block
 
     def score_part(c):
-        window, here = place(c)
-        st_buf[c % 2] = lax.dot_general(kk[window], q_ref[here], NT, preferred_element_type=f32)
+        here, base = slice(c * rows, (c + 1) * rows), c // per_block * BLK
+        st_buf[c % 2, base:] = lax.dot_general(k[base:], q_ref[here], NT, preferred_element_type=f32)
 
     def dprob_part(c):
-        window, here = place(c)
-        dp_buf[c % 2] = lax.dot_general(vv[window], g_ref[here], NT, preferred_element_type=f32)
+        here, base = slice(c * rows, (c + 1) * rows), c // per_block * BLK
+        dp_buf[c % 2, base:] = lax.dot_general(v[base:], g_ref[here], NT, preferred_element_type=f32)
+
+    def parts(c):
+        found = []
+        for o in range(BACK + 1):
+            place, j = divmod(c // per_block + o, BLK_DEV)
+            if place == 0:
+                found.append((e_buf.at[c % 2], dp_buf.at[c % 2], None, None, j))
+            elif place == 1:
+                found.append((e1_ref.at[c], dp1_ref.at[c], top1_ref, sum1_ref, j))
+            else:
+                found.append((e0_ref.at[c], dp0_ref.at[c], top0_ref, sum0_ref, j))
+        return found
 
     def exp_part(c):
-        st = st_buf.at[c % 2]
+        tops, sums = [], []
+        for _, _, top_ref, sum_ref, j in parts(c):
+            if top_ref is None:
+                e, top, total = block_scores(st_buf[c % 2, SPANS[j]], factor)
+                e_buf[c % 2, SPANS[j]] = e
+            else:
+                top, total = top_ref[c, j:j + 1], sum_ref[c, j:j + 1]
+            tops.append(top)
+            sums.append(total)
         shut = off[c // per_block]
-        key = lax.broadcasted_iota(jnp.int32, (BLK, rows), 0) * heads
-        row = lax.broadcasted_iota(jnp.int32, (BLK, rows), 1) + c % per_block * rows
-        own = jnp.where(key <= row, st[SPANS[BACK]], -OFF)
-        top = jnp.max(own, axis=0, keepdims=True)
-        for o in range(BACK):
-            top = jnp.maximum(top, jnp.max(st[SPANS[o]], axis=0, keepdims=True) - shut[o])
-        shift = top * factor
-        total = jnp.zeros((1, rows), f32)
-        for o in range(BACK + 1):
-            if o == BACK:
-                e = jnp.exp2(own * factor - shift)
-            else:
-                e = jnp.exp2(st[SPANS[o]] * factor - (shift + shut[o]))
-            total = total + jnp.sum(e, axis=0, keepdims=True)
-            st[SPANS[o]] = e
-        return 1.0 / total
-
-    def near(c):
-        return BACK - c // per_block
-
-    def prob_part(c, inv):
-        st, dp = st_buf.at[c % 2], dp_buf.at[c % 2]
+        tops = [t if s is None else t - s for t, s in zip(tops, shut)]
+        top = functools.reduce(jnp.maximum, tops)
+        shares = [jnp.exp2(t - top) for t in tops]
+        inv = 1.0 / functools.reduce(jnp.add, [a * b for a, b in zip(shares, sums)])
+        return [share * inv for share in shares]
+
+    def prob_part(c, shares):
         delta = jnp.zeros((1, rows), f32)
-        for o in range(BACK + 1):
-            p_low = (st[SPANS[o]] * inv).astype(low)
-            if o < near(c):
+        for o, (e, dp, _, _, j) in enumerate(parts(c)):
+            p_low = (e[SPANS[j]] * shares[o]).astype(low)
+            if o < away(c):
                 p_buf[c % 2, SPANS[o]] = p_low
             else:
                 own_ref[c, SPANS[o - BACK + 1]] = p_low
-            delta = delta + jnp.sum(p_low.astype(f32) * dp[SPANS[o]], axis=0, keepdims=True)
+            delta = delta + jnp.sum(p_low.astype(f32) * dp[SPANS[j]], axis=0, keepdims=True)
         return delta
 
-    def dscore_part(c, inv, delta):
-        st, dp = st_buf.at[c % 2], dp_buf.at[c % 2]
-        for o in range(BACK + 1):
-            ds = st[SPANS[o]] * inv * (dp[SPANS[o]] - delta) * scale
+    def dscore_part(c, shares, delta):
+        for o, (e, dp, _, _, j) in enumerate(parts(c)):
+            ds = e[SPANS[j]] * shares[o] * (dp[SPANS[j]] - delta) * scale
             d_ref[c, SPANS[o]] = ds.astype(low)
 
     def value_part(c):
-        window, here = place(c)
-        count = near(c) * BLK
-        dv[window.start:far] += jnp.dot(p_buf[c % 2, :count], g_ref[here], preferred_element_type=f32)
+        here, base, size = slice(c * rows, (c + 1) * rows), c // per_block * BLK, away(c) * BLK
+        dv[base:far] += jnp.dot(p_buf[c % 2, :size], g_ref[here], preferred_element_type=f32)
 
     def key_part(c):
-        window, here = place(c)
-        count = near(c) * BLK
-        dk[window.start:far] += jnp.dot(d_ref[c, :count], q_ref[here], preferred_element_type=f32)
+        here, base, size = slice(c * rows, (c + 1) * rows), c // per_block * BLK, away(c) * BLK
+        dk[base:far] += jnp.dot(d_ref[c, :size], q_ref[here], preferred_element_type=f32)
 
     for c in range(-1, chunks + 1):
         first, inside, last = c + 1 < chunks, 0 <= c < chunks, c >= 1
         if first:
             score_part(c + 1)
         if inside:
-            inv = exp_part(c)
+            shares = exp_part(c)
         if last:
             value_part(c - 1)
         if first:
             dprob_part(c + 1)
         if inside:
-            delta = prob_part(c, inv)
+            delta = prob_part(c, shares)
         if last:
             key_part(c - 1)
         if inside:
-            dscore_part(c, inv, delta)
+            dscore_part(c, shares, delta)
     for i, ref in enumerate((y2_ref, y1_ref)):
-        k = dk[i * LOCAL:(i + 1) * LOCAL]
-        v = dv[i * LOCAL:(i + 1) * LOCAL]
-        ref[:, 0] = k.astype(low).reshape(ref.shape[0], -1, head_size)
-        ref[:, 1] = v.astype(low).reshape(ref.shape[0], -1, head_size)
+        dk_part = dk[i * LOCAL:(i + 1) * LOCAL]
+        dv_part = dv[i * LOCAL:(i + 1) * LOCAL]
+        ref[:, 0] = dk_part.astype(low).reshape(ref.shape[0], -1, head_size)
+        ref[:, 1] = dv_part.astype(low).reshape(ref.shape[0], -1, head_size)
 
 
 def finish_kernel(q_ref, g_ref, x0_ref, x1_ref, x2_ref, d_ref, own_ref,
@@ -214,38 +255,54 @@
     )(q, g)
 
 
-def remote_grads(prev, q, g, x0, x1, x2, heads, rows):
+def part_scores(q, g, x, heads, rows, own):
+    chunks = q.shape[0] // rows
+    f32 = jnp.float32
+    big = jax.ShapeDtypeStruct((chunks, LOCAL, rows), f32)
+    small = jax.ShapeDtypeStruct((chunks, 8, rows), f32)
+    return pl.pallas_call(
+        functools.partial(part_kernel, heads=heads, rows=rows, own=own),
+        out_shape=(big, big, small, small),
+        in_specs=[VMEM] * 3,
+        out_specs=(VMEM,) * 4,
+        scratch_shapes=[pltpu.VMEM((2, LOCAL, rows), f32)],
+        cost_estimate=pl.CostEstimate(
+            flops=2 * 2 * LOCAL * q.size, bytes_accessed=4 * q.size, transcendentals=LOCAL * q.shape[0]
+        ),
+        compiler_params=pltpu.CompilerParams(vmem_limit_bytes=4 << 20),
+        name="own_scores" if own else "near_scores",
+    )(q, g, x)
+
+
+def remote_grads(prev, q, g, x2, own, near, heads, rows):
     head_size = q.shape[1]
-    keys = 3 * LOCAL
     chunks = q.shape[0] // rows
     low = q.dtype
     f32 = jnp.float32
-    pairs = 2 * BACK + 2
     return pl.pallas_call(
         functools.partial(scores_kernel, heads=heads, rows=rows),
         out_shape=(
-            jax.ShapeDtypeStruct(x0.shape, low),
-            jax.ShapeDtypeStruct(x0.shape, low),
+            jax.ShapeDtypeStruct(x2.shape, low),
+            jax.ShapeDtypeStruct(x2.shape, low),
             jax.ShapeDtypeStruct((chunks, SPAN, rows), low),
             jax.ShapeDtypeStruct((chunks, LOCAL, rows), low),
         ),
-        in_specs=[SMEM] + [VMEM] * 5,
+        in_specs=[SMEM] + [VMEM] * 11,
         out_specs=(VMEM,) * 4,
         scratch_shapes=[
-            pltpu.VMEM((keys, head_size), low),
-            pltpu.VMEM((keys, head_size), low),
             pltpu.VMEM((2 * LOCAL, head_size), f32),
             pltpu.VMEM((2 * LOCAL, head_size), f32),
-            pltpu.VMEM((2, SPAN, rows), f32),
-            pltpu.VMEM((2, SPAN, rows), f32),
+            pltpu.VMEM((2, LOCAL, rows), f32),
+            pltpu.VMEM((2, LOCAL, rows), f32),
+            pltpu.VMEM((2, LOCAL, rows), f32),
             pltpu.VMEM((2, BACK * BLK, rows), low),
         ],
         cost_estimate=pl.CostEstimate(
             flops=2 * 4 * SPAN * q.size, bytes_accessed=8 * q.size, transcendentals=SPAN * q.shape[0]
         ),
-        compiler_params=pltpu.CompilerParams(vmem_limit_bytes=24 << 20),
+        compiler_params=pltpu.CompilerParams(vmem_limit_bytes=10 << 20),
         name="remote_grads",
-    )(prev, q, g, x0, x1, x2)
+    )(prev, q, g, x2, *own, *near)
 
 
 def own_grads(q, g, x0, x1, x2, d_low, own, pieces=4):
@@ -273,9 +330,11 @@
     )(q, g, x0, x1, x2, d_low, own)
 
 
-def local_grads(prev, q, g, x0, x1, x2, heads, rows=512):
-    y1, y2, d_low, own = remote_grads(prev, q, g, x0, x1, x2, heads, rows)
-    dq, y0 = own_grads(q, g, x0, x1, x2, d_low, own)
+def local_grads(prev, q, g, x0, x1, x2, heads, rows=256):
+    own = part_scores(q, g, x0, heads, rows, True)
+    near = part_scores(q, g, x1, heads, rows, False)
+    y1, y2, d_low, p_own = remote_grads(prev, q, g, x2, own, near, heads, rows)
+    dq, y0 = own_grads(q, g, x0, x1, x2, d_low, p_own)
     return dq, y0, y1, y2
 
 
@@ -304,10 +363,13 @@
         queries.reshape(tok_count * heads, head_size),
         output_gradient.reshape(tok_count * heads, head_size),
     )
-    y1, y2, d_low, own = remote_grads(prev, q, g, x0, x1, x2, heads, 256)
+    rows = 256
+    own = part_scores(q, g, x0, heads, rows, True)
+    near = part_scores(q, g, x1, heads, rows, False)
+    y1, y2, d_low, p_own = remote_grads(prev, q, g, x2, own, near, heads, rows)
     r2 = passed_along(y2, "ctx", -2)
     r1 = passed_along(y1, "ctx", -1)
-    dq, y0 = own_grads(q, g, x0, x1, x2, d_low, own)
+    dq, y0 = own_grads(q, g, x0, x1, x2, d_low, p_own)
     f32 = jnp.float32
     summed = (y0.astype(f32) + r1.astype(f32) + r2.astype(f32)).astype(low)
     back = lax.all_to_all(summed, "tp", split_axis=0, concat_axis=0, tiled=True)

time: 65.9 us -> 65.7 us (level)
  waiting for transfers between devices: 16.8 us -> 16 us
    ppermute x4, waiting for transfers between devices: 14.3 us -> 10.9 us  [passed_along(): return lax.ppermute(block, axis, route)]
    all_to_all x1, waiting for transfers between devices: 2.51 us -> 5.13 us  [on_device(): x0 = lax.all_to_all(packed, 'tp', split_axis=0, concat_axis=0, tiled=True)]
    pallas_call x0 -> x2, Pallas kernels: none -> 2.52 us  [part_scores(): pl.pallas_call(functools.partial(part_kernel, heads=heads, rows=rows, own...]
    pallas_call x1, Pallas kernels: 8.13 us -> 6.13 us  [remote_grads(): pl.pallas_call(functools.partial(scores_kernel, heads=heads, rows=rows),...]
  transfers between devices with their start and end apart: 5 -> 5, of which waited for: 4 -> 3; matrix products, arithmetic and copies ran while one was open for 1% -> 1% of each run, Pallas kernels for 4% -> 8%
where the time goes in v3:
time: 65.7 us; the launch traced here: 65.2 us
  starting transfers between devices  21 us (32%)
  waiting for transfers between devices  16 us (24%)
  Pallas kernels  14.9 us (23%)
  blocking collectives  9.16 us (14%)
  local copies, waits for them, and re-layouts  2.44 us (4%)
  other arithmetic  1.01 us (2%)
  between operations  0.74 us (1%)
    ppermute x4, starting transfers between devices, passed_along(): return lax.ppermute(block, axis, route)  16.5 us
    ppermute x4, waiting for transfers between devices, passed_along(): return lax.ppermute(block, axis, route)  10.9 us
    all_to_all x1, blocking collectives, on_device(): back = lax.all_to_all(summed, 'tp', split_axis=0, concat_axis=0, tiled=True)  9.16 us
    pallas_call x1, Pallas kernels, remote_grads(): pl.pallas_call(functools.partial(scores_kernel, heads=heads, rows=rows),...  6.13 us
    all_to_all x1, waiting for transfers between devices, on_device(): x0 = lax.all_to_all(packed, 'tp', split_axis=0, concat_axis=0, tiled=True)  5.13 us
    all_to_all x1, starting transfers between devices, on_device(): x0 = lax.all_to_all(packed, 'tp', split_axis=0, concat_axis=0, tiled=True)  4.47 us
    pallas_call x1, Pallas kernels, own_grads(): pl.pallas_call(functools.partial(finish_kernel, rows=rows, pieces=pieces)...  2.54 us
    pallas_call x2, Pallas kernels, part_scores(): pl.pallas_call(functools.partial(part_kernel, heads=heads, rows=rows, own...  2.52 us
  transfers between devices with their start and end apart: 5, of which 3 were waited for; matrix products, arithmetic and copies ran while one was open for 1% of the time, Pallas kernels for 8%

profile of v3, /device:TPU:6, one launch (start us, length us, event | category | flops | bytes accessed | tf_op | source)
XLA Modules:
  0.0 65.2 jit_solution(5386046072914860673)
XLA Ops:
  0.6 1.8 %to_groups.1 = bf16[8,2,32,128]{3,2,1,0:T(8,128)(2,1)} custom-call(bf16[32,8,128]{2,1,0:T(8,128)(2,1)} %k_ref.1, bf16[32,8,128]{2,1,0:T(8,128)(2,1)} %v_ref.1), custom_call_target="tpu_custom_call" | custom-call | tf_op jit(solution)/shard_map/to_groups/pallas_call | solution.py:345
  2.4 4.5 %all-to-all-start = ((bf16[8,2,32,128]{3,2,1,0:T(8,128)(2,1)}), bf16[8,2,32,128]{3,2,1,0:T(8,128)(2,1)S(1)}, u32[]{:S(2)}, u32[]{:S(2)}) async-start(bf16[8,2,32,128]{3,2,1,0:T(8,128)(2,1)} %to_groups.1), calls=%async_computation | async-start | bytes 262144 | tf_op jit(solution)/shard_map/all_to_all | solution.py:353
  6.9 0.8 %select_reduce_fusion = s32[64]{0:T(128)S(1)} fusion(s32[64]{0:T(128)} %param.9), kind=kLoop, calls=%fused_computation.1 | loop fusion | flops 12224 | bytes 512 | tf_op jit(solution)/shard_map/reduce_sum | solution.py:358
  7.7 0.2 fusion
  7.9 5.1 %all-to-all-done.x_ref.x0_ref = bf16[8,2,32,128]{3,2,1,0:T(8,128)(2,1)S(1)} async-done(((bf16[8,2,32,128]{3,2,1,0:T(8,128)(2,1)}), bf16[8,2,32,128]{3,2,1,0:T(8,128)(2,1)S(1)}, u32[]{:S(2)}, u32[]{:S(2)}) %all-to-all-start) | async-done | bytes 131104 | tf_op jit(solution)/shard_map/all_to_all | solution.py:353
  13.0 5.2 %collective-permute-start.1 = (bf16[8,2,32,128]{3,2,1,0:T(8,128)(2,1)S(1)}, bf16[8,2,32,128]{3,2,1,0:T(8,128)(2,1)S(1)}, u32[]{:S(2)}, u32[]{:S(2)}) collective-permute-start(bf16[8,2,32,128]{3,2,1,0:T(8,128)(2,1)S(1)} %all-to-all-done.x_ref.x0_ref), channel_id=1, source_target_pairs={{0,16},{8,24},{16,32},{24,40},{32,48},{40,56},{48,64},{56,72},{64,... | collective-permute-start | bytes 393224 | tf_op jit(solution)/shard_map/ppermute | solution.py:25
  18.2 3.8 %collective-permute-start = (bf16[8,2,32,128]{3,2,1,0:T(8,128)(2,1)S(1)}, bf16[8,2,32,128]{3,2,1,0:T(8,128)(2,1)S(1)}, u32[]{:S(2)}, u32[]{:S(2)}) collective-permute-start(bf16[8,2,32,128]{3,2,1,0:T(8,128)(2,1)S(1)} %all-to-all-done.x_ref.x0_ref), channel_id=1, source_target_pairs={{0,8},{8,16},{16,24},{24,32},{32,40},{40,48},{48,56},{56,64},{64,7... | collective-permute-start | bytes 393224 | tf_op jit(solution)/shard_map/ppermute | solution.py:25
  22.0 0.0 copy-start
  22.1 1.2 %copy-done = bf16[256,16,128]{2,1,0:T(8,128)(2,1)S(1)} copy-done((bf16[256,16,128]{2,1,0:T(8,128)(2,1)S(1)}, bf16[256,16,128]{2,1,0:T(8,128)(2,1)}, u32[]{:S(2)}) %copy-start) | copy-done | bytes 1048600
  23.3 0.0 copy-start.1
  23.3 1.2 %copy-done.1 = bf16[256,16,128]{2,1,0:T(8,128)(2,1)S(1)} copy-done((bf16[256,16,128]{2,1,0:T(8,128)(2,1)S(1)}, bf16[256,16,128]{2,1,0:T(8,128)(2,1)}, u32[]{:S(2)}) %copy-start.1) | copy-done | bytes 1048600
  24.5 0.2 stage.1
  24.7 1.2 %own_scores.1 = (f32[16,256,256]{2,1,0:T(8,128)S(1)}, f32[16,256,256]{2,1,0:T(8,128)S(1)}, f32[16,8,256]{2,1,0:T(8,128)S(1)}, f32[16,8,256]{2,1,0:T(8,128)S(1)}) custom-call(bf16[4096,128]{1,0:T(8,128)(2,1)S(1)} %get-tuple-element.21.q_ref, bf16[4096,128]{1,0:T(8,128)(2,1)S(1)} %get-tuple-element.22.g_ref, bf16[8,2,32,128]{3,2,1,0:T(8,128)(2,1)S(1)} %all-to-all-done.x_ref.x0_ref), custom_call_target="tpu_custom_call" | custom-call | flops 536870912 | bytes 2097152 | tf_op jit(solution)/shard_map/own_scores/pallas_call | solution.py:263
  25.8 7.7 %collective-permute-done.x_ref.x1_ref = bf16[8,2,32,128]{3,2,1,0:T(8,128)(2,1)S(1)} collective-permute-done((bf16[8,2,32,128]{3,2,1,0:T(8,128)(2,1)S(1)}, bf16[8,2,32,128]{3,2,1,0:T(8,128)(2,1)S(1)}, u32[]{:S(2)}, u32[]{:S(2)}) %collective-permute-start) | collective-permute-done | bytes 131104 | tf_op jit(solution)/shard_map/ppermute | solution.py:25
  33.6 1.3 %near_scores.1 = (f32[16,256,256]{2,1,0:T(8,128)S(1)}, f32[16,256,256]{2,1,0:T(8,128)S(1)}, f32[16,8,256]{2,1,0:T(8,128)S(1)}, f32[16,8,256]{2,1,0:T(8,128)S(1)}) custom-call(bf16[4096,128]{1,0:T(8,128)(2,1)S(1)} %get-tuple-element.21.q_ref, bf16[4096,128]{1,0:T(8,128)(2,1)S(1)} %get-tuple-element.22.g_ref, ...), custom_call_target="tpu_custom_call" | custom-call | flops 536870912 | bytes 2097152 | tf_op jit(solution)/shard_map/near_scores/pallas_call | solution.py:263
  34.9 0.0 collective-permute-done.1.x2_ref
  34.9 6.1 %remote_grads.1 = (bf16[8,2,32,128]{3,2,1,0:T(8,128)(2,1)S(1)}, bf16[8,2,32,128]{3,2,1,0:T(8,128)(2,1)S(1)}, bf16[16,640,256]{2,1,0:T(8,128)(2,1)S(1)}, bf16[16,256,256]{2,1,0:T(8,128)(2,1)S(1)}) custom-call(s32[2]{0:T(128)S(1)} %fusion.1.prev_ref, bf16[4096,128]{1,0:T(8,128)(2,1)S(1)} %get-tuple-element.21.q_ref, ...), custom_call_target="tpu_custom_call" | custom-call | flops 2684354560 | bytes 4194304 | tf_op jit(solution)/shard_map/remote_grads/pallas_call | solution.py:282
  41.1 3.0 %collective-permute-start.2 = (bf16[8,2,32,128]{3,2,1,0:T(8,128)(2,1)S(1)}, bf16[8,2,32,128]{3,2,1,0:T(8,128)(2,1)S(1)}, u32[]{:S(2)}, u32[]{:S(2)}) collective-permute-start(bf16[8,2,32,128]{3,2,1,0:T(8,128)(2,1)S(1)} %get-tuple-element.35), channel_id=1, source_target_pairs={{8,0},{16,8},{24,16},{32,24},{40,32},{48,40},{56,48},{64,56},{72,6... | collective-permute-start | bytes 393224 | tf_op jit(solution)/shard_map/ppermute | solution.py:25
  44.0 4.5 %collective-permute-start.3 = (bf16[8,2,32,128]{3,2,1,0:T(8,128)(2,1)S(1)}, bf16[8,2,32,128]{3,2,1,0:T(8,128)(2,1)S(1)}, u32[]{:S(2)}, u32[]{:S(2)}) collective-permute-start(bf16[8,2,32,128]{3,2,1,0:T(8,128)(2,1)S(1)} %get-tuple-element.36), channel_id=1, source_target_pairs={{16,0},{24,8},{32,16},{40,24},{48,32},{56,40},{64,48},{72,56},{80,... | collective-permute-start | bytes 393224 | tf_op jit(solution)/shard_map/ppermute | solution.py:25
  48.6 2.5 %own_grads.1 = (bf16[4096,128]{1,0:T(8,128)(2,1)}, bf16[8,2,32,128]{3,2,1,0:T(8,128)(2,1)S(1)}) custom-call(bf16[4096,128]{1,0:T(8,128)(2,1)S(1)} %get-tuple-element.21.q_ref, bf16[4096,128]{1,0:T(8,128)(2,1)S(1)} %get-tuple-element.22.g_ref, bf16[8,2,32,128]{3,2,1,0:T(8,128)(2,1)S(1)} %all-to-all-done.x_ref.x0_ref, ...), custom_call_target="tpu_custom_call" | custom-call | flops 1342177280 | bytes 4194304 | tf_op jit(solution)/shard_map/own_grads/pallas_call | solution.py:313
  51.1 0.0 collective-permute-done.2
  51.1 3.1 %collective-permute-done.3 = bf16[8,2,32,128]{3,2,1,0:T(8,128)(2,1)S(1)} collective-permute-done((bf16[8,2,32,128]{3,2,1,0:T(8,128)(2,1)S(1)}, bf16[8,2,32,128]{3,2,1,0:T(8,128)(2,1)S(1)}, u32[]{:S(2)}, u32[]{:S(2)}) %collective-permute-start.3) | collective-permute-done | bytes 131104 | tf_op jit(solution)/shard_map/ppermute | solution.py:25
  54.3 0.1 add_convert_fusion
  54.4 9.2 %all_to_all.10.in_ref = bf16[8,2,32,128]{3,2,1,0:T(8,128)(2,1)} all-to-all(bf16[8,2,32,128]{3,2,1,0:T(8,128)(2,1)S(1)} %add_convert_fusion), channel_id=1, replica_groups=mesh['ctx'=64,'tp'=8] {'tp'}, dimensions={0} | all-to-all | bytes 262144 | tf_op jit(solution)/shard_map/all_to_all | solution.py:375
  63.5 1.7 %from_groups.1 = (bf16[32,8,128]{2,1,0:T(8,128)(2,1)}, bf16[32,8,128]{2,1,0:T(8,128)(2,1)}) custom-call(bf16[8,2,32,128]{3,2,1,0:T(8,128)(2,1)} %all_to_all.10.in_ref), custom_call_target="tpu_custom_call" | custom-call | tf_op jit(solution)/shard_map/from_groups/pallas_call | solution.py:376
  (2 shorter events, 0.0 us)
Async XLA Ops:
  2.4 10.6 %all-to-all-start = ((bf16[8,2,32,128]{3,2,1,0:T(8,128)(2,1)}), bf16[8,2,32,128]{3,2,1,0:T(8,128)(2,1)S(1)}, u32[]{:S(2)}, u32[]{:S(2)}) async-start(bf16[8,2,32,128]{3,2,1,0:T(8,128)(2,1)} %to_groups.1), calls=%async_computation | async-start | bytes 262144 | tf_op jit(solution)/shard_map/all_to_all | solution.py:353
  13.0 21.9 %collective-permute-start.1 = (bf16[8,2,32,128]{3,2,1,0:T(8,128)(2,1)S(1)}, bf16[8,2,32,128]{3,2,1,0:T(8,128)(2,1)S(1)}, u32[]{:S(2)}, u32[]{:S(2)}) collective-permute-start(bf16[8,2,32,128]{3,2,1,0:T(8,128)(2,1)S(1)} %all-to-all-done.x_ref.x0_ref), channel_id=1, source_target_pairs={{0,16},{8,24},{16,32},{24,40},{32,48},{40,56},{48,64},{56,72},{64,... | collective-permute-start | bytes 393224 | tf_op jit(solution)/shard_map/ppermute | solution.py:25
  18.2 15.4 %collective-permute-start = (bf16[8,2,32,128]{3,2,1,0:T(8,128)(2,1)S(1)}, bf16[8,2,32,128]{3,2,1,0:T(8,128)(2,1)S(1)}, u32[]{:S(2)}, u32[]{:S(2)}) collective-permute-start(bf16[8,2,32,128]{3,2,1,0:T(8,128)(2,1)S(1)} %all-to-all-done.x_ref.x0_ref), channel_id=1, source_target_pairs={{0,8},{8,16},{16,24},{24,32},{32,40},{40,48},{48,56},{56,64},{64,7... | collective-permute-start | bytes 393224 | tf_op jit(solution)/shard_map/ppermute | solution.py:25
  22.0 1.2 %copy-start = (bf16[256,16,128]{2,1,0:T(8,128)(2,1)S(1)}, bf16[256,16,128]{2,1,0:T(8,128)(2,1)}, u32[]{:S(2)}) copy-start(bf16[256,16,128]{2,1,0:T(8,128)(2,1)} %param.5) | copy-start | bytes 3145732
  23.3 1.2 %copy-start.1 = (bf16[256,16,128]{2,1,0:T(8,128)(2,1)S(1)}, bf16[256,16,128]{2,1,0:T(8,128)(2,1)}, u32[]{:S(2)}) copy-start(bf16[256,16,128]{2,1,0:T(8,128)(2,1)} %param.8) | copy-start | bytes 3145732
  41.1 10.1 %collective-permute-start.2 = (bf16[8,2,32,128]{3,2,1,0:T(8,128)(2,1)S(1)}, bf16[8,2,32,128]{3,2,1,0:T(8,128)(2,1)S(1)}, u32[]{:S(2)}, u32[]{:S(2)}) collective-permute-start(bf16[8,2,32,128]{3,2,1,0:T(8,128)(2,1)S(1)} %get-tuple-element.35), channel_id=1, source_target_pairs={{8,0},{16,8},{24,16},{32,24},{40,32},{48,40},{56,48},{64,56},{72,6... | collective-permute-start | bytes 393224 | tf_op jit(solution)/shard_map/ppermute | solution.py:25
  44.0 10.2 %collective-permute-start.3 = (bf16[8,2,32,128]{3,2,1,0:T(8,128)(2,1)S(1)}, bf16[8,2,32,128]{3,2,1,0:T(8,128)(2,1)S(1)}, u32[]{:S(2)}, u32[]{:S(2)}) collective-permute-start(bf16[8,2,32,128]{3,2,1,0:T(8,128)(2,1)S(1)} %get-tuple-element.36), channel_id=1, source_target_pairs={{16,0},{24,8},{32,16},{40,24},{48,32},{56,40},{64,48},{72,56},{80,... | collective-permute-start | bytes 393224 | tf_op jit(solution)/shard_map/ppermute | solution.py:25

commit v4 on v3

--- a/solution.py
+++ b/solution.py
@@ -7,6 +7,7 @@
 from jax.experimental import pallas as pl
 from jax.experimental.pallas import tpu as pltpu
 from jax.sharding import PartitionSpec as P
+
 
 BLK = 128
 BLK_DEV = 2
@@ -328,14 +329,6 @@
         compiler_params=pltpu.CompilerParams(vmem_limit_bytes=16 << 20),
         name="own_grads",
     )(q, g, x0, x1, x2, d_low, own)
-
-
-def local_grads(prev, q, g, x0, x1, x2, heads, rows=256):
-    own = part_scores(q, g, x0, heads, rows, True)
-    near = part_scores(q, g, x1, heads, rows, False)
-    y1, y2, d_low, p_own = remote_grads(prev, q, g, x2, own, near, heads, rows)
-    dq, y0 = own_grads(q, g, x0, x1, x2, d_low, p_own)
-    return dq, y0, y1, y2
 
 
 def on_device(queries, keys, values, output_gradient, doc_blocks):

time: 65.7 us -> 65.7 us (level)
  no operation moved by 1% of the time
where the time goes in v4:
time: 65.7 us; the launch traced here: 65.2 us
  starting transfers between devices  21 us (32%)
  waiting for transfers between devices  16 us (24%)
  Pallas kernels  14.9 us (23%)
  blocking collectives  9.16 us (14%)
  local copies, waits for them, and re-layouts  2.44 us (4%)
  other arithmetic  1.01 us (2%)
  between operations  0.74 us (1%)
    ppermute x4, starting transfers between devices, passed_along(): return lax.ppermute(block, axis, route)  16.5 us
    ppermute x4, waiting for transfers between devices, passed_along(): return lax.ppermute(block, axis, route)  10.9 us
    all_to_all x1, blocking collectives, on_device(): back = lax.all_to_all(summed, 'tp', split_axis=0, concat_axis=0, tiled=True)  9.16 us
    pallas_call x1, Pallas kernels, remote_grads(): pl.pallas_call(functools.partial(scores_kernel, heads=heads, rows=rows),...  6.13 us
    all_to_all x1, waiting for transfers between devices, on_device(): x0 = lax.all_to_all(packed, 'tp', split_axis=0, concat_axis=0, tiled=True)  5.13 us
    all_to_all x1, starting transfers between devices, on_device(): x0 = lax.all_to_all(packed, 'tp', split_axis=0, concat_axis=0, tiled=True)  4.47 us
    pallas_call x1, Pallas kernels, own_grads(): pl.pallas_call(functools.partial(finish_kernel, rows=rows, pieces=pieces)...  2.54 us
    pallas_call x2, Pallas kernels, part_scores(): pl.pallas_call(functools.partial(part_kernel, heads=heads, rows=rows, own...  2.52 us
  transfers between devices with their start and end apart: 5, of which 3 were waited for; matrix products, arithmetic and copies ran while one was open for 1% of the time, Pallas kernels for 8%

profile of v4, /device:TPU:6, one launch (start us, length us, event | category | flops | bytes accessed | tf_op | source)
XLA Modules:
  0.0 65.2 jit_solution(5386046072914860673)
XLA Ops:
  0.6 1.8 %to_groups.1 = bf16[8,2,32,128]{3,2,1,0:T(8,128)(2,1)} custom-call(bf16[32,8,128]{2,1,0:T(8,128)(2,1)} %k_ref.1, bf16[32,8,128]{2,1,0:T(8,128)(2,1)} %v_ref.1), custom_call_target="tpu_custom_call" | custom-call | tf_op jit(solution)/shard_map/to_groups/pallas_call | solution.py:338
  2.4 4.5 %all-to-all-start = ((bf16[8,2,32,128]{3,2,1,0:T(8,128)(2,1)}), bf16[8,2,32,128]{3,2,1,0:T(8,128)(2,1)S(1)}, u32[]{:S(2)}, u32[]{:S(2)}) async-start(bf16[8,2,32,128]{3,2,1,0:T(8,128)(2,1)} %to_groups.1), calls=%async_computation | async-start | bytes 262144 | tf_op jit(solution)/shard_map/all_to_all | solution.py:346
  6.9 0.8 %select_reduce_fusion = s32[64]{0:T(128)S(1)} fusion(s32[64]{0:T(128)} %param.9), kind=kLoop, calls=%fused_computation.1 | loop fusion | flops 12224 | bytes 512 | tf_op jit(solution)/shard_map/reduce_sum | solution.py:351
  7.7 0.2 fusion
  7.9 5.1 %all-to-all-done.x_ref.x0_ref = bf16[8,2,32,128]{3,2,1,0:T(8,128)(2,1)S(1)} async-done(((bf16[8,2,32,128]{3,2,1,0:T(8,128)(2,1)}), bf16[8,2,32,128]{3,2,1,0:T(8,128)(2,1)S(1)}, u32[]{:S(2)}, u32[]{:S(2)}) %all-to-all-start) | async-done | bytes 131104 | tf_op jit(solution)/shard_map/all_to_all | solution.py:346
  13.0 5.2 %collective-permute-start.1 = (bf16[8,2,32,128]{3,2,1,0:T(8,128)(2,1)S(1)}, bf16[8,2,32,128]{3,2,1,0:T(8,128)(2,1)S(1)}, u32[]{:S(2)}, u32[]{:S(2)}) collective-permute-start(bf16[8,2,32,128]{3,2,1,0:T(8,128)(2,1)S(1)} %all-to-all-done.x_ref.x0_ref), channel_id=1, source_target_pairs={{0,16},{8,24},{16,32},{24,40},{32,48},{40,56},{48,64},{56,72},{64,... | collective-permute-start | bytes 393224 | tf_op jit(solution)/shard_map/ppermute | solution.py:26
  18.2 3.8 %collective-permute-start = (bf16[8,2,32,128]{3,2,1,0:T(8,128)(2,1)S(1)}, bf16[8,2,32,128]{3,2,1,0:T(8,128)(2,1)S(1)}, u32[]{:S(2)}, u32[]{:S(2)}) collective-permute-start(bf16[8,2,32,128]{3,2,1,0:T(8,128)(2,1)S(1)} %all-to-all-done.x_ref.x0_ref), channel_id=1, source_target_pairs={{0,8},{8,16},{16,24},{24,32},{32,40},{40,48},{48,56},{56,64},{64,7... | collective-permute-start | bytes 393224 | tf_op jit(solution)/shard_map/ppermute | solution.py:26
  22.0 0.0 copy-start
  22.1 1.2 %copy-done = bf16[256,16,128]{2,1,0:T(8,128)(2,1)S(1)} copy-done((bf16[256,16,128]{2,1,0:T(8,128)(2,1)S(1)}, bf16[256,16,128]{2,1,0:T(8,128)(2,1)}, u32[]{:S(2)}) %copy-start) | copy-done | bytes 1048600
  23.3 0.0 copy-start.1
  23.3 1.2 %copy-done.1 = bf16[256,16,128]{2,1,0:T(8,128)(2,1)S(1)} copy-done((bf16[256,16,128]{2,1,0:T(8,128)(2,1)S(1)}, bf16[256,16,128]{2,1,0:T(8,128)(2,1)}, u32[]{:S(2)}) %copy-start.1) | copy-done | bytes 1048600
  24.5 0.2 stage.1
  24.7 1.2 %own_scores.1 = (f32[16,256,256]{2,1,0:T(8,128)S(1)}, f32[16,256,256]{2,1,0:T(8,128)S(1)}, f32[16,8,256]{2,1,0:T(8,128)S(1)}, f32[16,8,256]{2,1,0:T(8,128)S(1)}) custom-call(bf16[4096,128]{1,0:T(8,128)(2,1)S(1)} %get-tuple-element.21.q_ref, bf16[4096,128]{1,0:T(8,128)(2,1)S(1)} %get-tuple-element.22.g_ref, bf16[8,2,32,128]{3,2,1,0:T(8,128)(2,1)S(1)} %all-to-all-done.x_ref.x0_ref), custom_call_target="tpu_custom_call" | custom-call | flops 536870912 | bytes 2097152 | tf_op jit(solution)/shard_map/own_scores/pallas_call | solution.py:264
  25.8 7.7 %collective-permute-done.x_ref.x1_ref = bf16[8,2,32,128]{3,2,1,0:T(8,128)(2,1)S(1)} collective-permute-done((bf16[8,2,32,128]{3,2,1,0:T(8,128)(2,1)S(1)}, bf16[8,2,32,128]{3,2,1,0:T(8,128)(2,1)S(1)}, u32[]{:S(2)}, u32[]{:S(2)}) %collective-permute-start) | collective-permute-done | bytes 131104 | tf_op jit(solution)/shard_map/ppermute | solution.py:26
  33.6 1.3 %near_scores.1 = (f32[16,256,256]{2,1,0:T(8,128)S(1)}, f32[16,256,256]{2,1,0:T(8,128)S(1)}, f32[16,8,256]{2,1,0:T(8,128)S(1)}, f32[16,8,256]{2,1,0:T(8,128)S(1)}) custom-call(bf16[4096,128]{1,0:T(8,128)(2,1)S(1)} %get-tuple-element.21.q_ref, bf16[4096,128]{1,0:T(8,128)(2,1)S(1)} %get-tuple-element.22.g_ref, ...), custom_call_target="tpu_custom_call" | custom-call | flops 536870912 | bytes 2097152 | tf_op jit(solution)/shard_map/near_scores/pallas_call | solution.py:264
  34.9 0.0 collective-permute-done.1.x2_ref
  34.9 6.1 %remote_grads.1 = (bf16[8,2,32,128]{3,2,1,0:T(8,128)(2,1)S(1)}, bf16[8,2,32,128]{3,2,1,0:T(8,128)(2,1)S(1)}, bf16[16,640,256]{2,1,0:T(8,128)(2,1)S(1)}, bf16[16,256,256]{2,1,0:T(8,128)(2,1)S(1)}) custom-call(s32[2]{0:T(128)S(1)} %fusion.1.prev_ref, bf16[4096,128]{1,0:T(8,128)(2,1)S(1)} %get-tuple-element.21.q_ref, ...), custom_call_target="tpu_custom_call" | custom-call | flops 2684354560 | bytes 4194304 | tf_op jit(solution)/shard_map/remote_grads/pallas_call | solution.py:283
  41.1 3.0 %collective-permute-start.2 = (bf16[8,2,32,128]{3,2,1,0:T(8,128)(2,1)S(1)}, bf16[8,2,32,128]{3,2,1,0:T(8,128)(2,1)S(1)}, u32[]{:S(2)}, u32[]{:S(2)}) collective-permute-start(bf16[8,2,32,128]{3,2,1,0:T(8,128)(2,1)S(1)} %get-tuple-element.35), channel_id=1, source_target_pairs={{8,0},{16,8},{24,16},{32,24},{40,32},{48,40},{56,48},{64,56},{72,6... | collective-permute-start | bytes 393224 | tf_op jit(solution)/shard_map/ppermute | solution.py:26
  44.0 4.5 %collective-permute-start.3 = (bf16[8,2,32,128]{3,2,1,0:T(8,128)(2,1)S(1)}, bf16[8,2,32,128]{3,2,1,0:T(8,128)(2,1)S(1)}, u32[]{:S(2)}, u32[]{:S(2)}) collective-permute-start(bf16[8,2,32,128]{3,2,1,0:T(8,128)(2,1)S(1)} %get-tuple-element.36), channel_id=1, source_target_pairs={{16,0},{24,8},{32,16},{40,24},{48,32},{56,40},{64,48},{72,56},{80,... | collective-permute-start | bytes 393224 | tf_op jit(solution)/shard_map/ppermute | solution.py:26
  48.6 2.5 %own_grads.1 = (bf16[4096,128]{1,0:T(8,128)(2,1)}, bf16[8,2,32,128]{3,2,1,0:T(8,128)(2,1)S(1)}) custom-call(bf16[4096,128]{1,0:T(8,128)(2,1)S(1)} %get-tuple-element.21.q_ref, bf16[4096,128]{1,0:T(8,128)(2,1)S(1)} %get-tuple-element.22.g_ref, bf16[8,2,32,128]{3,2,1,0:T(8,128)(2,1)S(1)} %all-to-all-done.x_ref.x0_ref, ...), custom_call_target="tpu_custom_call" | custom-call | flops 1342177280 | bytes 4194304 | tf_op jit(solution)/shard_map/own_grads/pallas_call | solution.py:314
  51.1 0.0 collective-permute-done.2
  51.1 3.1 %collective-permute-done.3 = bf16[8,2,32,128]{3,2,1,0:T(8,128)(2,1)S(1)} collective-permute-done((bf16[8,2,32,128]{3,2,1,0:T(8,128)(2,1)S(1)}, bf16[8,2,32,128]{3,2,1,0:T(8,128)(2,1)S(1)}, u32[]{:S(2)}, u32[]{:S(2)}) %collective-permute-start.3) | collective-permute-done | bytes 131104 | tf_op jit(solution)/shard_map/ppermute | solution.py:26
  54.3 0.1 add_convert_fusion
  54.4 9.2 %all_to_all.10.in_ref = bf16[8,2,32,128]{3,2,1,0:T(8,128)(2,1)} all-to-all(bf16[8,2,32,128]{3,2,1,0:T(8,128)(2,1)S(1)} %add_convert_fusion), channel_id=1, replica_groups=mesh['ctx'=64,'tp'=8] {'tp'}, dimensions={0} | all-to-all | bytes 262144 | tf_op jit(solution)/shard_map/all_to_all | solution.py:368
  63.5 1.7 %from_groups.1 = (bf16[32,8,128]{2,1,0:T(8,128)(2,1)}, bf16[32,8,128]{2,1,0:T(8,128)(2,1)}) custom-call(bf16[8,2,32,128]{3,2,1,0:T(8,128)(2,1)} %all_to_all.10.in_ref), custom_call_target="tpu_custom_call" | custom-call | tf_op jit(solution)/shard_map/from_groups/pallas_call | solution.py:369
  (2 shorter events, 0.0 us)
Async XLA Ops:
  2.4 10.6 %all-to-all-start = ((bf16[8,2,32,128]{3,2,1,0:T(8,128)(2,1)}), bf16[8,2,32,128]{3,2,1,0:T(8,128)(2,1)S(1)}, u32[]{:S(2)}, u32[]{:S(2)}) async-start(bf16[8,2,32,128]{3,2,1,0:T(8,128)(2,1)} %to_groups.1), calls=%async_computation | async-start | bytes 262144 | tf_op jit(solution)/shard_map/all_to_all | solution.py:346
  13.0 21.9 %collective-permute-start.1 = (bf16[8,2,32,128]{3,2,1,0:T(8,128)(2,1)S(1)}, bf16[8,2,32,128]{3,2,1,0:T(8,128)(2,1)S(1)}, u32[]{:S(2)}, u32[]{:S(2)}) collective-permute-start(bf16[8,2,32,128]{3,2,1,0:T(8,128)(2,1)S(1)} %all-to-all-done.x_ref.x0_ref), channel_id=1, source_target_pairs={{0,16},{8,24},{16,32},{24,40},{32,48},{40,56},{48,64},{56,72},{64,... | collective-permute-start | bytes 393224 | tf_op jit(solution)/shard_map/ppermute | solution.py:26
  18.2 15.4 %collective-permute-start = (bf16[8,2,32,128]{3,2,1,0:T(8,128)(2,1)S(1)}, bf16[8,2,32,128]{3,2,1,0:T(8,128)(2,1)S(1)}, u32[]{:S(2)}, u32[]{:S(2)}) collective-permute-start(bf16[8,2,32,128]{3,2,1,0:T(8,128)(2,1)S(1)} %all-to-all-done.x_ref.x0_ref), channel_id=1, source_target_pairs={{0,8},{8,16},{16,24},{24,32},{32,40},{40,48},{48,56},{56,64},{64,7... | collective-permute-start | bytes 393224 | tf_op jit(solution)/shard_map/ppermute | solution.py:26
  22.0 1.2 %copy-start = (bf16[256,16,128]{2,1,0:T(8,128)(2,1)S(1)}, bf16[256,16,128]{2,1,0:T(8,128)(2,1)}, u32[]{:S(2)}) copy-start(bf16[256,16,128]{2,1,0:T(8,128)(2,1)} %param.5) | copy-start | bytes 3145732
  23.3 1.2 %copy-start.1 = (bf16[256,16,128]{2,1,0:T(8,128)(2,1)S(1)}, bf16[256,16,128]{2,1,0:T(8,128)(2,1)}, u32[]{:S(2)}) copy-start(bf16[256,16,128]{2,1,0:T(8,128)(2,1)} %param.8) | copy-start | bytes 3145732
  41.1 10.1 %collective-permute-start.2 = (bf16[8,2,32,128]{3,2,1,0:T(8,128)(2,1)S(1)}, bf16[8,2,32,128]{3,2,1,0:T(8,128)(2,1)S(1)}, u32[]{:S(2)}, u32[]{:S(2)}) collective-permute-start(bf16[8,2,32,128]{3,2,1,0:T(8,128)(2,1)S(1)} %get-tuple-element.35), channel_id=1, source_target_pairs={{8,0},{16,8},{24,16},{32,24},{40,32},{48,40},{56,48},{64,56},{72,6... | collective-permute-start | bytes 393224 | tf_op jit(solution)/shard_map/ppermute | solution.py:26
  44.0 10.2 %collective-permute-start.3 = (bf16[8,2,32,128]{3,2,1,0:T(8,128)(2,1)S(1)}, bf16[8,2,32,128]{3,2,1,0:T(8,128)(2,1)S(1)}, u32[]{:S(2)}, u32[]{:S(2)}) collective-permute-start(bf16[8,2,32,128]{3,2,1,0:T(8,128)(2,1)S(1)} %get-tuple-element.36), channel_id=1, source_target_pairs={{16,0},{24,8},{32,16},{40,24},{48,32},{56,40},{64,48},{72,56},{80,... | collective-permute-start | bytes 393224 | tf_op jit(solution)/shard_map/ppermute | solution.py:26
